TPU v7x, 32 devices: a whole 2x2x4 slice. The times are simulated.
32 devices in a mesh: groups: 2 (over x), rows: 8 (over z, y), chan: 2 (over core).
Axes of the slice: x: 2, y: 2, z: 4, core: 2. Of those that a mesh axis runs over, the one named last changes fastest.
Arguments:
- latents: bfloat16 [48, 32, 1024], P('groups', 'rows', 'chan'), parts along dimension 0, may hold values from -6 to 6
- timestep: int32 [6], P('groups'), parts along dimension 0, may hold values from 0 to 999
- label: int32 [6], P('groups'), parts along dimension 0, may hold values from 0 to 15
- time_table: bfloat16 [1000, 1024], P(None, 'chan'), may hold values from -3 to 3
- class_table: bfloat16 [16, 1024], replicated, may hold values from -6 to 6
- dw_kernel: bfloat16 [7, 7, 1024], P(None, None, 'chan'), may hold values from -0.875 to 0.875
- dw_bias: bfloat16 [1024], P('chan'), may hold values from -3 to 3
- ln_gain: bfloat16 [1024], P('chan'), may hold values from 0.25 to 1.75
- ln_bias: bfloat16 [1024], P('chan'), may hold values from -2 to 2
- up_weight: bfloat16 [1024, 4096], P(None, 'chan'), may hold values from -0.1875 to 0.1875
- up_bias: bfloat16 [4096], P('chan'), may hold values from -3 to 3
- down_weight: bfloat16 [4096, 1024], P('chan'), may hold values from -0.09375 to 0.09375
- down_bias: bfloat16 [1024], P('chan'), may hold values from -3 to 3
- layer_scale: bfloat16 [1024], replicated, may hold values from 0.5 to 1.5
Outputs:
- features: bfloat16 [48, 32, 1024], P(('groups', 'rows'), None, 'chan'), parts along dimension 0
- gradient: float32 [48, 32, 1024], P('groups', 'rows', 'chan'), parts along dimension 0
There are 2 independent parts, one for each index of `groups`. A program takes and returns all parts, laid end to end along the dimension named above; an argument that names none is the same for every part. Nothing has to cross between parts.
Inputs may be any that keep to these rules, and one draw needn't show every extreme that they name: One timestep index for each image, a row of the table of 1000 timesteps. `label`: one defect class for each image, out of 16 classes.
All inputs are finite; a program needn't handle non-finite values.
Results may differ from a plain program's by a relative error of at most 0.0045.
Values may be sent and summed in bfloat16 or wider, within the bound.
No kernel may reach another device: no remote copies, remote signals or barrier semaphores. Data moves between devices by JAX's collectives and lax.ppermute only.
A program may use at most 128 MiB of HBM per device.

v0:
```python
import jax
import jax.numpy as jnp
from jax import lax
from jax.sharding import PartitionSpec as P

KAPPA = 0.7978845608028654
EPSILON = 1e-06


def with_halo(cells, sides, width):
    for axis, dim in sides:
        count = lax.axis_size(axis)
        ends = count - 1
        head = lax.slice_in_dim(cells, 0, width, axis=dim)
        tail = lax.slice_in_dim(cells, cells.shape[dim] - width, cells.shape[dim], axis=dim)
        cells = jnp.concatenate(
            [
                lax.ppermute(tail, axis, [(i, (i + 1) % count) for i in range(ends)]),
                cells,
                lax.ppermute(head, axis, [((i + 1) % count, i) for i in range(ends)]),
            ],
            axis=dim,
        )
    return cells


def gelu_tanh(values):
    inner = KAPPA * (values + 0.044715 * values * values * values)
    return 0.5 * values * (1.0 + jnp.tanh(inner))


def gelu_slope(values):
    tangent = jnp.tanh(KAPPA * (values + 0.044715 * values * values * values))
    return 0.5 * (1.0 + tangent) + 0.5 * values * (1.0 - tangent * tangent) * KAPPA * (
        1.0 + 3.0 * 0.044715 * values * values
    )


def stencil(padded, kernel, masks):
    height = padded.shape[0] - 6
    width = padded.shape[1] - 6
    total = jnp.zeros((height, width, padded.shape[2]), jnp.float32)
    for row_tap in range(7):
        partial_row = jnp.zeros((height, width, padded.shape[2]), jnp.float32)
        for col_tap in range(7):
            partial_row = (
                partial_row
                + padded[row_tap : row_tap + height, col_tap : col_tap + width, :]
                * kernel[row_tap, col_tap]
            )
        total = total + partial_row * masks[row_tap][:, None, None]
    return total


def exact_dot(left, right):
    return jnp.dot(left, right, precision=lax.Precision.HIGHEST, preferred_element_type=jnp.float32)


def local_block(
    latent_pad,
    row_first,
    col_first,
    total_rows,
    total_cols,
    pad_grad,
    time_rows,
    class_half,
    slope_image,
    scale_half,
    dw_kernel,
    dw_bias,
    ln_gain,
    ln_bias,
    up_weight,
    up_bias,
    down_weight,
    down_bias,
    full_channels,
):
    pad_rows = latent_pad.shape[0]
    pad_cols = latent_pad.shape[1]
    height = pad_rows - 6
    width = pad_cols - 6
    channels = latent_pad.shape[2]
    images = time_rows.shape[0]
    image_height = total_rows // images
    row_global = row_first - 3 + jnp.arange(pad_rows, dtype=jnp.int32)
    row_image = jnp.floor_divide(row_global, image_height)
    col_global = col_first - 3 + jnp.arange(pad_cols, dtype=jnp.int32)
    col_valid = ((col_global >= 0) & (col_global < total_cols)).astype(jnp.float32)
    image_hot = (row_image[:, None] == jnp.arange(images, dtype=jnp.int32)[None, :]).astype(
        jnp.float32
    )
    time_pad = exact_dot(image_hot, time_rows)
    start_pad = latent_pad.astype(jnp.float32) + time_pad[:, None, :] * col_valid[None, :, None]
    masks = jnp.stack(
        [
            (row_image[tap : tap + height] == row_image[3 : 3 + height]).astype(jnp.float32)
            for tap in range(7)
        ]
    )
    kernel = dw_kernel.astype(jnp.float32)
    mixed = stencil(start_pad, kernel, masks) + dw_bias.astype(jnp.float32)
    tokens = height * width
    flat = mixed.reshape(tokens, channels)
    first_sum, second_sum = lax.psum((jnp.sum(flat, 1), jnp.sum(flat * flat, 1)), "chan")
    mean = first_sum / full_channels
    variance = second_sum / full_channels - mean * mean
    inverse = lax.rsqrt(variance + EPSILON)
    normed = (flat - mean[:, None]) * inverse[:, None]
    gain = ln_gain.astype(jnp.float32)
    scaled = (normed * gain + ln_bias.astype(jnp.float32)).astype(jnp.bfloat16)
    hidden = jnp.dot(
        lax.all_gather(scaled, "chan", axis=1, tiled=True),
        up_weight,
        preferred_element_type=jnp.float32,
    )
    hidden = hidden + up_bias.astype(jnp.float32)
    active = gelu_tanh(hidden).astype(jnp.bfloat16)
    branch = lax.psum_scatter(
        jnp.dot(active, down_weight, preferred_element_type=jnp.float32),
        "chan",
        scatter_dimension=1,
        tiled=True,
    )
    branch = branch + down_bias.astype(jnp.float32)
    start_cells = start_pad[3 : 3 + height, 3 : 3 + width].reshape(tokens, channels)
    features = (
        (start_cells + scale_half * branch).astype(jnp.bfloat16).reshape(height, width, channels)
    )
    token_image = image_hot[3 : 3 + height]
    slope_rows = exact_dot(token_image, slope_image)
    slope_tokens = jnp.broadcast_to(
        slope_rows[:, None, :], (height, width, slope_rows.shape[1])
    ).reshape(tokens, slope_rows.shape[1])
    hidden_grad = (slope_tokens * gelu_slope(hidden)).astype(jnp.bfloat16)
    grad_terms = lax.dot_general(
        hidden_grad, up_weight, (((1,), (1,)), ((), ())), preferred_element_type=jnp.float32
    )
    normed_grad = lax.psum_scatter(
        grad_terms.astype(jnp.bfloat16), "chan", scatter_dimension=1, tiled=True
    ).astype(jnp.float32)
    gained = normed_grad * gain
    grad_first, grad_second = lax.psum((jnp.sum(gained, 1), jnp.sum(gained * normed, 1)), "chan")
    mixed_grad = inverse[:, None] * (
        gained - grad_first[:, None] / full_channels - normed * grad_second[:, None] / full_channels
    )
    grad_pad = pad_grad(mixed_grad.reshape(height, width, channels))
    class_tokens = exact_dot(token_image, class_half)
    gradient = stencil(grad_pad, kernel[::-1, ::-1], masks) + class_tokens[:, None, :]
    return (features, gradient)


def per_device(
    latents,
    timestep,
    label,
    time_table,
    class_table,
    dw_kernel,
    dw_bias,
    ln_gain,
    ln_bias,
    up_weight,
    up_bias,
    down_weight,
    down_bias,
    layer_scale,
):
    channels = ln_gain.shape[0]
    full_channels = class_table.shape[1]
    half_index = lax.axis_index("chan")
    scale_full = layer_scale.astype(jnp.float32)
    scale_half = lax.dynamic_slice_in_dim(scale_full, half_index * channels, channels, 0)
    time_hot = (
        timestep[:, None] == jnp.arange(time_table.shape[0], dtype=jnp.int32)[None, :]
    ).astype(jnp.float32)
    time_rows = exact_dot(time_hot, time_table.astype(jnp.float32))
    class_hot = (
        label[:, None] == jnp.arange(class_table.shape[0], dtype=jnp.int32)[None, :]
    ).astype(jnp.float32)
    class_rows = exact_dot(class_hot, class_table.astype(jnp.float32))
    class_half = lax.dynamic_slice_in_dim(class_rows, half_index * channels, channels, 1)
    direction = (class_rows * scale_full).astype(jnp.bfloat16)
    slope_image = lax.dot_general(
        direction, down_weight, (((1,), (1,)), ((), ())), preferred_element_type=jnp.float32
    )
    latent_rows = lax.all_to_all(latents, "rows", split_axis=0, concat_axis=1, tiled=True)
    height = latent_rows.shape[0]
    width = latent_rows.shape[1]
    row_first = lax.axis_index("rows") * height
    col_first = 0
    total_rows = height * lax.axis_size("rows")
    latent_pad = with_halo(latent_rows, (("rows", 0),), 3)
    latent_pad = jnp.pad(latent_pad, ((0, 0), (3, 3), (0, 0)))

    def pad_grad(field):
        padded = with_halo(field.astype(jnp.bfloat16), (("rows", 0),), 3).astype(field.dtype)
        return jnp.pad(padded, ((0, 0), (3, 3), (0, 0)))

    features, gradient = local_block(
        latent_pad,
        row_first,
        col_first,
        total_rows,
        width,
        pad_grad,
        time_rows,
        class_half,
        slope_image,
        scale_half,
        dw_kernel,
        dw_bias,
        ln_gain,
        ln_bias,
        up_weight,
        up_bias,
        down_weight,
        down_bias,
        full_channels,
    )
    gradient = lax.all_to_all(gradient, "rows", split_axis=1, concat_axis=0, tiled=True)
    return (features, gradient)


def solution(mesh):
    in_specs = (
        P("groups", "rows", "chan"),
        P("groups"),
        P("groups"),
        P(None, "chan"),
        P(),
        P(None, None, "chan"),
        P("chan"),
        P("chan"),
        P("chan"),
        P(None, "chan"),
        P("chan"),
        P("chan", None),
        P("chan"),
        P(),
    )
    out_specs = (P(("groups", "rows"), None, "chan"), P("groups", "rows", "chan"))
    return jax.shard_map(
        per_device, mesh=mesh, in_specs=in_specs, out_specs=out_specs, check_vma=False
    )
```

profile of v0, /device:TPU:0, one launch (start us, length us, event | category | flops | bytes accessed | tf_op | source)
XLA Modules:
  0.0 107.5 jit_solution(14234665979605698154)
XLA Ops:
  7.2 7.5 %all-to-all-start = ((bf16[24,4,512]{2,1,0:T(4,128)(2,1)}), bf16[24,4,512]{2,1,0:T(4,128)(2,1)S(1)}, u32[]{:S(2)}, u32[]{:S(2)}) async-start(bf16[24,4,512]{2,1,0:T(4,128)(2,1)} %param.14), calls=%async_computation | async-start | bytes 196608 | tf_op jit(solution)/shard_map/all_to_all | solution.py:188
  15.8 1.1 %fusion.183 = (f32[1,1,512]{2,1,0:T(1,128)S(1)}, f32[1,1,512]{2,1,0:T(1,128)S(1)}, f32[1,1,512]{2,1,0:T(1,128)S(1)}, f32[1,1,512]{2,1,0:T(1,128)S(1)}, f32[1,1,5...) fusion(bf16[7,7,512]{2,1,0:T(8,128)(2,1)} %param.19), kind=kLoop, calls=%fused_computation.314 | loop fusion | bytes 77824 | tf_op jit(solution)/shard_map/slice | solution.py:49
  17.1 1.6 %fusion.182 = (f32[1,1,512]{2,1,0:T(1,128)S(1)}, f32[1,1,512]{2,1,0:T(1,128)S(1)}, f32[1,1,512]{2,1,0:T(1,128)S(1)}, f32[1,1,512]{2,1,0:T(1,128)S(1)}, f32[1,1,5...) fusion(bf16[7,7,512]{2,1,0:T(8,128)(2,1)} %param.19), kind=kLoop, calls=%fused_computation.313 | loop fusion | bytes 77824 | tf_op jit(solution)/shard_map/slice | solution.py:49
  23.7 3.4 %fusion.164 = f32[3,2048]{1,0:T(4,128)S(1)} fusion(bf16[2048,1024]{1,0:T(8,128)(2,1)} %param.25, f32[3,1024]{1,0:T(4,128)S(1)} %fusion.169, f32[1024]{0:T(1024)S(1)} %convert_element_type.93), kind=kOutput, calls=%fused_computation.280 | convolution fusion | flops 12589056 | bytes 4235264 | tf_op jit(solution)/shard_map/dot_general | solution.py:185
  28.0 1.3 %collective-permute-start.1 = (bf16[3,32,512]{2,0,1:T(4,128)(2,1)S(1)}, bf16[3,32,512]{2,0,1:T(4,128)(2,1)S(1)}, u32[]{:S(2)}, u32[]{:S(2)}) collective-permute-start(bf16[3,32,512]{2,0,1:T(4,128)(2,1)S(1)} %bitcast.86), channel_id=1, source_target_pairs={{2,0},{4,2},{6,4},{8,6},{10,8},{12,10},{14,12},{3,1},{5,3},{7,5},{... | collective-permute-start | bytes 294920 | tf_op jit(solution)/shard_map/ppermute | solution.py:20
  29.3 4.6 %collective-permute-start = (bf16[3,32,512]{2,0,1:T(4,128)(2,1)S(1)}, bf16[3,32,512]{2,0,1:T(4,128)(2,1)S(1)}, u32[]{:S(2)}, u32[]{:S(2)}) collective-permute-start(bf16[3,32,512]{2,0,1:T(4,128)(2,1)S(1)} %bitcast.87), channel_id=1, source_target_pairs={{0,2},{2,4},{4,6},{6,8},{8,10},{10,12},{12,14},{1,3},{3,5},{5,7},{... | collective-permute-start | bytes 294920 | tf_op jit(solution)/shard_map/ppermute | solution.py:18
  33.9 1.0 collective-permute-done.1
  34.9 2.9 %collective-permute-done = bf16[3,32,512]{2,0,1:T(4,128)(2,1)S(1)} collective-permute-done((bf16[3,32,512]{2,0,1:T(4,128)(2,1)S(1)}, bf16[3,32,512]{2,0,1:T(4,128)(2,1)S(1)}, u32[]{:S(2)}, u32[]{:S(2)}) %collective-permute-start) | collective-permute-done | bytes 98336 | tf_op jit(solution)/shard_map/ppermute | solution.py:18
  38.6 5.1 %fusion.180 = (f32[3,32]{0,1:T(8,128)S(1)}, f32[3,32]{0,1:T(8,128)S(1)}, f32[3,32,512]{2,0,1:T(4,128)S(1)}) fusion(f32[512]{0:T(512)S(1)} %convert_element_type.101, f32[3]{0:T(128)} %get-tuple-element.67, f32[512]{0:T(512)S(1)} %bitcast.113, f32[9,38,512]{2,0,1:T(8,128)S(1)} %multiply_add_fusion, f32[512]{0:T(512)S(1)} %bitcast.111, f32[512]{0:T(512)S(1)} %bitcast.109, ...), kind=kLoop, calls=%fused_computation.312 | loop fusion | flops 5259072 | bytes 9933640 | tf_op jit(solution)/shard_map/reduce_sum | solution.py:106
  44.0 2.5 %all-reduce.3 = (f32[96]{0:T(128)S(1)}, f32[96]{0:T(128)S(1)}) all-reduce(f32[96]{0:T(128)S(1)} %reduce_sum.43, f32[96]{0:T(128)S(1)} %reduce_sum.41), channel_id=1, replica_groups=mesh['groups'=2,'rows'=8,'chan'=2] {'chan'}, use_global_device_ids=true, to_apply=%region_3.4 | all-reduce | flops 192 | bytes 1536 | tf_op jit(solution)/shard_map/psum | solution.py:106
  46.6 1.9 %all_gather.3 = bf16[96,1024]{1,0:T(8,128)(2,1)S(1)} all-gather(bf16[96,512]{1,0:T(8,128)(2,1)S(1)} %add_convert_fusion), channel_id=1, replica_groups=mesh['groups'=2,'rows'=8,'chan'=2] {'chan'}, dimensions={1}, use_global_device_ids=true | all-gather | bytes 294912 | tf_op jit(solution)/shard_map/all_gather | solution.py:114
  48.6 3.6 %fusion.7 = (bf16[96,2048]{1,0:T(8,128)(2,1)S(1)}, f32[96,2048]{1,0:T(8,128)S(1)}) fusion(f32[3,2048]{1,0:T(4,128)S(1)} %fusion.171, f32[2048]{0:T(1024)S(1)} %convert_element_type.105, bf16[96,1024]{1,0:T(8,128)(2,1)S(1)} %all_gather.3, bf16[1024,2048]{1,0:T(8,128)(2,1)} %param.23), kind=kOutput, calls=%fused_computation.56 | convolution fusion | flops 406585344 | bytes 5603328 | tf_op jit(solution)/shard_map/dot_general | solution.py:113
  52.2 2.1 %convolution_convert_fusion = bf16[96,1024]{1,0:T(8,128)(2,1)} fusion(bf16[96,2048]{1,0:T(8,128)(2,1)S(1)} %get-tuple-element.68, bf16[1024,2048]{1,0:T(8,128)(2,1)S(1)} %copy-done.1), kind=kOutput, calls=%fused_computation.49 | convolution fusion | flops 402751488 | bytes 4784128 | tf_op jit(solution)/shard_map/dot_general | solution.py:137
  54.5 9.4 %reduce-scatter.5.cloned.1.call-done = bf16[96,512]{1,0:T(8,128)(2,1)} async-done(((bf16[96,1024]{1,0:T(8,128)(2,1)}), bf16[96,512]{1,0:T(8,128)(2,1)}) %reduce-scatter.5.cloned.1.call-update) | async-done | bytes 98320 | tf_op jit(solution)/shard_map/reduce_scatter | solution.py:140
  63.9 1.1 %fusion.162 = (f32[96]{0:T(128)S(1)}, f32[96]{0:T(128)S(1)}) fusion(bf16[96,512]{1,0:T(8,128)(2,1)} %reduce-scatter.5.cloned.1.call-done, f32[512]{0:T(512)S(1)} %convert_element_type.102, f32[96]{0:T(128)S(1)} %get-tuple-element.61, f32[96]{0:T(128)S(1)} %get-tuple-element.60, f32[3,32,512]{2,1,0:T(8,128)S(1)} %copy.27), kind=kLoop, calls=%fused_computation.275 | loop fusion | flops 343872 | bytes 298496 | tf_op jit(solution)/shard_map/reduce_sum | solution.py:144
  65.0 2.5 %all-reduce.2 = (f32[96]{0:T(128)S(1)}, f32[96]{0:T(128)S(1)}) all-reduce(f32[96]{0:T(128)S(1)} %get-tuple-element.5, f32[96]{0:T(128)S(1)} %get-tuple-element.4), channel_id=1, replica_groups=mesh['groups'=2,'rows'=8,'chan'=2] {'chan'}, use_global_device_ids=true, to_apply=%region_9.10 | all-reduce | flops 192 | bytes 1536 | tf_op jit(solution)/shard_map/psum | solution.py:144
  67.5 1.0 multiply_convert_fusion.2
  68.6 1.3 %collective-permute-start.3 = (bf16[3,32,512]{2,0,1:T(4,128)(2,1)S(1)}, bf16[3,32,512]{2,0,1:T(4,128)(2,1)S(1)}, u32[]{:S(2)}, u32[]{:S(2)}) collective-permute-start(bf16[3,32,512]{2,0,1:T(4,128)(2,1)S(1)} %copy.30), channel_id=1, source_target_pairs={{2,0},{4,2},{6,4},{8,6},{10,8},{12,10},{14,12},{3,1},{5,3},{7,5},{... | collective-permute-start | bytes 294920 | tf_op jit(solution)/shard_map/ppermute | solution.py:20
  69.9 4.6 %collective-permute-start.2 = (bf16[3,32,512]{2,0,1:T(4,128)(2,1)S(1)}, bf16[3,32,512]{2,0,1:T(4,128)(2,1)S(1)}, u32[]{:S(2)}, u32[]{:S(2)}) collective-permute-start(bf16[3,32,512]{2,0,1:T(4,128)(2,1)S(1)} %copy.30), channel_id=1, source_target_pairs={{0,2},{2,4},{4,6},{6,8},{8,10},{10,12},{12,14},{1,3},{3,5},{5,7},{... | collective-permute-start | bytes 294920 | tf_op jit(solution)/shard_map/ppermute | solution.py:18
  74.5 3.8 %fusion.13 = f32[96,1024]{1,0:T(8,128)} fusion(bf16[2048,1024]{1,0:T(8,128)(2,1)} %param.25, f32[96,2048]{1,0:T(8,128)S(1)} %get-tuple-element.69), kind=kOutput, calls=%fused_computation.64 | convolution fusion | flops 404422656 | bytes 5373952 | tf_op jit(solution)/shard_map/dot_general | solution.py:121
  79.9 5.3 %add_add_fusion = f32[3,32,512]{2,0,1:T(4,128)} fusion(f32[9,32,512]{2,0,1:T(8,128)S(1)} %maximum_convert_fusion, f32[3,512]{1,0:T(4,128)S(1)} %fusion.165, f32[3]{0:T(128)} %get-tuple-element.67, f32[512]{0:T(512)S(1)} %bitcast.114, f32[512]{0:T(512)S(1)} %bitcast.112, f32[512]{0:T(512)S(1)} %bitcast.110, f32[512]{0:T(512)S(1)} %bitcast.108, ...), kind=kLoop, calls=%fused_computation.266 | loop fusion | flops 5111808 | bytes 3188808 | tf_op jit(solution)/shard_map/add | solution.py:150
  85.2 5.9 %all-to-all-start.1 = ((f32[3,32,512]{2,0,1:T(4,128)}), f32[3,32,512]{2,0,1:T(4,128)S(1)}, u32[]{:S(2)}, u32[]{:S(2)}) async-start(f32[3,32,512]{2,0,1:T(4,128)} %add_add_fusion), calls=%async_computation.3 | async-start | bytes 524288 | tf_op jit(solution)/shard_map/all_to_all | solution.py:222
  92.1 1.6 %fusion.161 = bf16[96,512]{1,0:T(8,128)(2,1)} fusion(f32[3,32,512]{2,1,0:T(8,128)S(1)} %copy.26, f32[96,512]{1,0:T(8,128)} %reduce-scatter.3.cloned.1.call-done, f32[512]{0:T(512)S(1)} %convert_element_type.107, f32[512]{0:T(512)S(1)} %dynamic_slice.6), kind=kLoop, calls=%fused_computation.271 | loop fusion | flops 196608 | bytes 495616 | tf_op jit(solution)/shard_map/convert_element_type | solution.py:129
  93.7 6.3 %all-to-all-done.1 = f32[3,32,512]{2,0,1:T(4,128)S(1)} async-done(((f32[3,32,512]{2,0,1:T(4,128)}), f32[3,32,512]{2,0,1:T(4,128)S(1)}, u32[]{:S(2)}, u32[]{:S(2)}) %all-to-all-start.1) | async-done | bytes 196640 | tf_op jit(solution)/shard_map/all_to_all | solution.py:222
  (206 shorter events, 10.7 us)
Async XLA Ops:
  7.2 20.8 %all-to-all-start = ((bf16[24,4,512]{2,1,0:T(4,128)(2,1)}), bf16[24,4,512]{2,1,0:T(4,128)(2,1)S(1)}, u32[]{:S(2)}, u32[]{:S(2)}) async-start(bf16[24,4,512]{2,1,0:T(4,128)(2,1)} %param.14), calls=%async_computation | async-start | bytes 196608 | tf_op jit(solution)/shard_map/all_to_all | solution.py:188
  14.7 49.3 %reduce-scatter.5.cloned.1.call-start = ((), (), s32[]{:S(2)}) async-start(), calls=%async_computation.5 | async-start | bytes 294912 | tf_op jit(solution)/shard_map/reduce_scatter | solution.py:140
  15.7 22.5 %copy-start.2 = (f32[1,1,512]{2,1,0:T(1,128)}, f32[1,1,512]{2,1,0:T(1,128)S(1)}, u32[]{:S(2)}) copy-start(f32[1,1,512]{2,1,0:T(1,128)S(1)} %get-tuple-element.51) | copy-start | bytes 6148
  15.7 22.5 %copy-start.4 = (f32[1,1,512]{2,1,0:T(1,128)}, f32[1,1,512]{2,1,0:T(1,128)S(1)}, u32[]{:S(2)}) copy-start(f32[1,1,512]{2,1,0:T(1,128)S(1)} %get-tuple-element.52) | copy-start | bytes 6148
  15.7 22.5 %copy-start.6 = (f32[1,1,512]{2,1,0:T(1,128)}, f32[1,1,512]{2,1,0:T(1,128)S(1)}, u32[]{:S(2)}) copy-start(f32[1,1,512]{2,1,0:T(1,128)S(1)} %get-tuple-element.53) | copy-start | bytes 6148
  15.7 22.5 %copy-start.8 = (f32[1,1,512]{2,1,0:T(1,128)}, f32[1,1,512]{2,1,0:T(1,128)S(1)}, u32[]{:S(2)}) copy-start(f32[1,1,512]{2,1,0:T(1,128)S(1)} %get-tuple-element.54) | copy-start | bytes 6148
  15.7 22.5 %copy-start.10 = (f32[1,1,512]{2,1,0:T(1,128)}, f32[1,1,512]{2,1,0:T(1,128)S(1)}, u32[]{:S(2)}) copy-start(f32[1,1,512]{2,1,0:T(1,128)S(1)} %get-tuple-element.55) | copy-start | bytes 6148
  15.7 22.5 %copy-start.12 = (f32[1,1,512]{2,1,0:T(1,128)}, f32[1,1,512]{2,1,0:T(1,128)S(1)}, u32[]{:S(2)}) copy-start(f32[1,1,512]{2,1,0:T(1,128)S(1)} %get-tuple-element.56) | copy-start | bytes 6148
  15.7 22.5 %copy-start.14 = (f32[1,1,512]{2,1,0:T(1,128)}, f32[1,1,512]{2,1,0:T(1,128)S(1)}, u32[]{:S(2)}) copy-start(f32[1,1,512]{2,1,0:T(1,128)S(1)} %get-tuple-element.57) | copy-start | bytes 6148
  15.8 22.5 %copy-start.16 = (f32[1,1,512]{2,1,0:T(1,128)}, f32[1,1,512]{2,1,0:T(1,128)S(1)}, u32[]{:S(2)}) copy-start(f32[1,1,512]{2,1,0:T(1,128)S(1)} %get-tuple-element.58) | copy-start | bytes 6148
  15.8 22.5 %copy-start.18 = (f32[1,1,512]{2,1,0:T(1,128)}, f32[1,1,512]{2,1,0:T(1,128)S(1)}, u32[]{:S(2)}) copy-start(f32[1,1,512]{2,1,0:T(1,128)S(1)} %get-tuple-element.59) | copy-start | bytes 6148
  16.9 21.3 %copy-start.20 = (f32[1,1,512]{2,1,0:T(1,128)}, f32[1,1,512]{2,1,0:T(1,128)S(1)}, u32[]{:S(2)}) copy-start(f32[1,1,512]{2,1,0:T(1,128)S(1)} %get-tuple-element.30) | copy-start | bytes 6148
  16.9 21.3 %copy-start.22 = (f32[1,1,512]{2,1,0:T(1,128)}, f32[1,1,512]{2,1,0:T(1,128)S(1)}, u32[]{:S(2)}) copy-start(f32[1,1,512]{2,1,0:T(1,128)S(1)} %get-tuple-element.31) | copy-start | bytes 6148
  16.9 21.3 %copy-start.24 = (f32[1,1,512]{2,1,0:T(1,128)}, f32[1,1,512]{2,1,0:T(1,128)S(1)}, u32[]{:S(2)}) copy-start(f32[1,1,512]{2,1,0:T(1,128)S(1)} %get-tuple-element.32) | copy-start | bytes 6148
  16.9 21.3 %copy-start.26 = (f32[1,1,512]{2,1,0:T(1,128)}, f32[1,1,512]{2,1,0:T(1,128)S(1)}, u32[]{:S(2)}) copy-start(f32[1,1,512]{2,1,0:T(1,128)S(1)} %get-tuple-element.33) | copy-start | bytes 6148
  17.0 21.3 %copy-start.28 = (f32[1,1,512]{2,1,0:T(1,128)}, f32[1,1,512]{2,1,0:T(1,128)S(1)}, u32[]{:S(2)}) copy-start(f32[1,1,512]{2,1,0:T(1,128)S(1)} %get-tuple-element.34) | copy-start | bytes 6148
  17.0 21.3 %copy-start.30 = (f32[1,1,512]{2,1,0:T(1,128)}, f32[1,1,512]{2,1,0:T(1,128)S(1)}, u32[]{:S(2)}) copy-start(f32[1,1,512]{2,1,0:T(1,128)S(1)} %get-tuple-element.35) | copy-start | bytes 6148
  17.0 21.3 %copy-start.32 = (f32[1,1,512]{2,1,0:T(1,128)}, f32[1,1,512]{2,1,0:T(1,128)S(1)}, u32[]{:S(2)}) copy-start(f32[1,1,512]{2,1,0:T(1,128)S(1)} %get-tuple-element.36) | copy-start | bytes 6148
  28.0 6.9 %collective-permute-start.1 = (bf16[3,32,512]{2,0,1:T(4,128)(2,1)S(1)}, bf16[3,32,512]{2,0,1:T(4,128)(2,1)S(1)}, u32[]{:S(2)}, u32[]{:S(2)}) collective-permute-start(bf16[3,32,512]{2,0,1:T(4,128)(2,1)S(1)} %bitcast.86), channel_id=1, source_target_pairs={{2,0},{4,2},{6,4},{8,6},{10,8},{12,10},{14,12},{3,1},{5,3},{7,5},{... | collective-permute-start | bytes 294920 | tf_op jit(solution)/shard_map/ppermute | solution.py:20
  29.3 8.5 %collective-permute-start = (bf16[3,32,512]{2,0,1:T(4,128)(2,1)S(1)}, bf16[3,32,512]{2,0,1:T(4,128)(2,1)S(1)}, u32[]{:S(2)}, u32[]{:S(2)}) collective-permute-start(bf16[3,32,512]{2,0,1:T(4,128)(2,1)S(1)} %bitcast.87), channel_id=1, source_target_pairs={{0,2},{2,4},{4,6},{6,8},{8,10},{10,12},{12,14},{1,3},{3,5},{5,7},{... | collective-permute-start | bytes 294920 | tf_op jit(solution)/shard_map/ppermute | solution.py:18
  54.3 37.8 %reduce-scatter.3.cloned.1.call-start = ((), (), s32[]{:S(2)}) async-start(), calls=%async_computation.4 | async-start | bytes 589824 | tf_op jit(solution)/shard_map/reduce_scatter | solution.py:120
  68.6 10.1 %collective-permute-start.3 = (bf16[3,32,512]{2,0,1:T(4,128)(2,1)S(1)}, bf16[3,32,512]{2,0,1:T(4,128)(2,1)S(1)}, u32[]{:S(2)}, u32[]{:S(2)}) collective-permute-start(bf16[3,32,512]{2,0,1:T(4,128)(2,1)S(1)} %copy.30), channel_id=1, source_target_pairs={{2,0},{4,2},{6,4},{8,6},{10,8},{12,10},{14,12},{3,1},{5,3},{7,5},{... | collective-permute-start | bytes 294920 | tf_op jit(solution)/shard_map/ppermute | solution.py:20
  69.9 9.3 %collective-permute-start.2 = (bf16[3,32,512]{2,0,1:T(4,128)(2,1)S(1)}, bf16[3,32,512]{2,0,1:T(4,128)(2,1)S(1)}, u32[]{:S(2)}, u32[]{:S(2)}) collective-permute-start(bf16[3,32,512]{2,0,1:T(4,128)(2,1)S(1)} %copy.30), channel_id=1, source_target_pairs={{0,2},{2,4},{4,6},{6,8},{8,10},{10,12},{12,14},{1,3},{3,5},{5,7},{... | collective-permute-start | bytes 294920 | tf_op jit(solution)/shard_map/ppermute | solution.py:18
  85.2 14.7 %all-to-all-start.1 = ((f32[3,32,512]{2,0,1:T(4,128)}), f32[3,32,512]{2,0,1:T(4,128)S(1)}, u32[]{:S(2)}, u32[]{:S(2)}) async-start(f32[3,32,512]{2,0,1:T(4,128)} %add_add_fusion), calls=%async_computation.3 | async-start | bytes 524288 | tf_op jit(solution)/shard_map/all_to_all | solution.py:222
  (67 other events, 582.4 us)
Sparse Core Ops, SparseCore 0:
  54.4 9.4 reduce-scatter.4
  78.8 8.9 reduce-scatter.2
where the time goes:
time: 109 us; the launch traced here: 108 us
  starting transfers between devices  25.1 us (23%)
  waiting for transfers between devices  20.2 us (19%)
  other arithmetic  19.8 us (18%)
  between operations  15.5 us (14%)
  matrix products  14.5 us (13%)
  blocking collectives  6.89 us (6%)
  local copies, waits for them, and re-layouts  5.62 us (5%)
    reduce_scatter x1, waiting for transfers between devices, local_block(): lax.psum_scatter(grad_terms.astype(jnp.bfloat16), 'chan', scatter_dimensi...  9.45 us
    ppermute x2, starting transfers between devices, with_halo(): lax.ppermute(tail, axis, [(i, (i + 1) % count) for i in range(ends)])  9.11 us
    all_to_all x1, starting transfers between devices, per_device(): lax.all_to_all(latents, 'rows', split_axis=0, concat_axis=1, tiled=True)  7.45 us
    all_to_all x1, waiting for transfers between devices, per_device(): lax.all_to_all(gradient, 'rows', split_axis=1, concat_axis=0, tiled=True)  6.28 us
    all_to_all x1, starting transfers between devices, per_device(): lax.all_to_all(gradient, 'rows', split_axis=1, concat_axis=0, tiled=True)  5.88 us
    add x1, other arithmetic, local_block(): stencil(grad_pad, kernel[::-1, ::-1], masks) + class_tokens[:, None, :]  5.34 us
    reduce_sum x1, other arithmetic, local_block(): jnp.sum(flat, 1)  5.05 us
    dot_general x1, matrix products, local_block(): jnp.dot(active, down_weight, preferred_element_type=jnp.float32)  3.82 us
  transfers between devices with their start and end apart: 8, of which 5 were waited for; matrix products, arithmetic and copies ran while one was open for 23% of the time, Pallas kernels for 0%

commit v1 on v0

v1 whole, which is shorter than its diff:
```python
import functools

import jax
import jax.numpy as jnp
from jax import lax
from jax.experimental import pallas as pl
from jax.experimental.pallas import tpu as pltpu
from jax.sharding import PartitionSpec as P

KAPPA = 0.7978845608028654
CUBIC = 0.044715
EPSILON = 1e-06
LANES = 128
MIB = 1 << 20


def call(body, outs, ins, scratch=(), limit=24, name=None, flops=0):
    specs = []
    args = []
    for item in ins:
        array, space = item if isinstance(item, tuple) else (item, pltpu.VMEM)
        specs.append(pl.BlockSpec(memory_space=space))
        args.append(array)
    return pl.pallas_call(
        body,
        out_shape=tuple(jax.ShapeDtypeStruct(s, d) for s, d in outs),
        in_specs=specs,
        out_specs=tuple(pl.BlockSpec(memory_space=pltpu.VMEM) for _ in outs),
        scratch_shapes=list(scratch),
        compiler_params=pltpu.CompilerParams(vmem_limit_bytes=limit * MIB),
        cost_estimate=pl.CostEstimate(flops=flops, transcendentals=0, bytes_accessed=0) if flops else None,
        name=name,
    )(*args)


def row_of(block, index):
    hit = lax.broadcasted_iota(jnp.int32, block.shape, 0) == index
    return jnp.sum(jnp.where(hit, block, 0.0), axis=0, keepdims=True)


def vec(ref):
    return ref[...].astype(jnp.float32).reshape(1, ref.shape[0])


def take(flat, first, count, stride):
    window = pl.ds(first, count, stride=stride) if stride > 1 else pl.ds(first, count)
    return jnp.concatenate([flat[l, window, :] for l in range(flat.shape[0])], axis=1)


def setup_kernel(
    timestep, label, time_table, class_table, layer_scale, down, time_out, class_out, slope_out, rows8, sems,
    *, images, half
):
    copies = []
    for i in range(images):
        base = pl.multiple_of((timestep[i] // 8) * 8, 8)
        copies.append(
            pltpu.make_async_copy(time_table.at[pl.ds(base, 8), :], rows8.at[i], sems.at[i])
        )
        copies[-1].start()
    mine = pl.multiple_of(lax.axis_index("chan") * half, half)
    scale = vec(layer_scale)
    table = class_table[...].astype(jnp.float32)
    table_half = class_table[:, pl.ds(mine, half)].astype(jnp.float32)
    full = [row_of(table, label[i]) for i in range(images)]
    for i in range(images):
        class_out[i : i + 1, :] = row_of(table_half, label[i])
    fill = [jnp.zeros_like(full[0])] * (8 - images)
    direction = (jnp.concatenate(full + fill, axis=0) * scale).astype(jnp.bfloat16)
    slope_out[...] = lax.dot_general(
        direction, down[...], (((1,), (1,)), ((), ())), preferred_element_type=jnp.float32
    )
    for i in range(images):
        copies[i].wait()
        time_out[i : i + 1, :] = row_of(rows8[i].astype(jnp.float32), timestep[i] % 8)


def stencil(cols, taps, store, flip, images, high, width):
    channels = cols.shape[2]
    row = lax.broadcasted_iota(jnp.int32, (high, LANES), 0)
    inside = [(row + (t - 3) >= 0) & (row + (t - 3) < high) for t in range(7)]
    for lane in range(0, channels, LANES):
        for image in range(images):
            first = image * high
            column = [cols[c, first : first + high, lane : lane + LANES] for c in range(width + 6)]
            total = [None] * width
            for t in range(7):
                part = [None] * width
                for d in range(7):
                    place = 8 * (6 - t) + 6 - d if flip else 8 * t + d
                    weight = jnp.broadcast_to(taps[place : place + 1, lane : lane + LANES], (high, LANES))
                    for c in range(width):
                        term = column[c + d] * weight
                        part[c] = term if d == 0 else part[c] + term
                for c in range(width):
                    moved = part[c]
                    if t != 3:
                        moved = pltpu.roll(moved, (3 - t) % high, 0)
                        moved = jnp.where(inside[t], moved, 0.0)
                    total[c] = moved if t == 0 else total[c] + moved
            for c in range(width):
                store(c, first, lane, total[c])


def load_taps(dw_kernel, taps):
    for t in range(7):
        taps[8 * t : 8 * t + 7, :] = dw_kernel[t].astype(jnp.float32)


def mix_kernel(
    own, left, right, time_rows, dw_kernel, dw_bias, gain, shift, mixed_out, start_out, flat, cols, taps,
    *, images, high, width
):
    rows = images * high
    position = lax.axis_index("rows")
    load_taps(dw_kernel, taps)
    for side, ref in enumerate((left, own, right)):
        for r in range(rows):
            cell = ref[r].astype(jnp.float32)
            for l in range(flat.shape[0]):
                flat[l, r * width : (r + 1) * width, :] = cell[:, l * LANES : (l + 1) * LANES]
        for c in range(width):
            place = (side - 1) * width + c + 3
            if place < 0 or place >= width + 6:
                continue
            for image in range(images):
                first = image * high
                value = take(flat, first * width + c, high, width) + time_rows[image : image + 1, :]
                if side == 0:
                    value = value * jnp.where(position > 0, 1.0, 0.0)
                if side == 2:
                    value = value * jnp.where(position < lax.axis_size("rows") - 1, 1.0, 0.0)
                cols[place, first : first + high, :] = value
                if side == 1:
                    start_out[c * rows + first : c * rows + first + high, :] = value
    bias = vec(dw_bias)

    def store(c, first, lane, value):
        mixed_out[c * rows + first : c * rows + first + high, lane : lane + LANES] = (
            value + bias[:, lane : lane + LANES]
        )

    stencil(cols, taps, store, False, images, high, width)
    tokens = rows * width
    mixed_out[tokens : tokens + 1, :] = vec(gain)
    mixed_out[tokens + 1 : tokens + 2, :] = vec(shift)


def mlp_kernel(
    own, other, slope, up, up_bias, down, branch_out, branch_send, grad_out, grad_send, sums_out, normed_out, inverse_out,
    active, hidden_grad, *, images, high, width, full, chunk
):
    tokens = images * high * width
    half = own.shape[1]
    hidden_size = up.shape[1]
    index = lax.axis_index("chan")
    mine = pl.multiple_of(index * half, half)
    theirs = pl.multiple_of((1 - index) * half, half)
    x = own[:tokens, :]
    y = other[:tokens, :]
    mean = (jnp.sum(x, 1, keepdims=True) + jnp.sum(y, 1, keepdims=True)) / full
    square = (jnp.sum(x * x, 1, keepdims=True) + jnp.sum(y * y, 1, keepdims=True)) / full
    inverse = lax.rsqrt(square - mean * mean + EPSILON)
    normed_x = (x - mean) * inverse
    normed_y = (y - mean) * inverse
    gain_x = own[tokens : tokens + 1, :]
    gain_y = other[tokens : tokens + 1, :]
    scaled_x = (normed_x * gain_x + own[tokens + 1 : tokens + 2, :]).astype(jnp.bfloat16)
    scaled_y = (normed_y * gain_y + other[tokens + 1 : tokens + 2, :]).astype(jnp.bfloat16)
    normed_out[...] = normed_x
    inverse_out[...] = jnp.broadcast_to(inverse, inverse_out.shape)
    bias = vec(up_bias)
    for j in range(0, hidden_size, chunk):
        hidden = jnp.dot(scaled_x, up[pl.ds(mine, half), j : j + chunk], preferred_element_type=jnp.float32)
        hidden = hidden + jnp.dot(
            scaled_y, up[pl.ds(theirs, half), j : j + chunk], preferred_element_type=jnp.float32
        )
        hidden = hidden + bias[:, j : j + chunk]
        cell = hidden * hidden
        tangent = jnp.tanh(KAPPA * (hidden + CUBIC * cell * hidden))
        grown = 0.5 * (1.0 + tangent)
        active[:, j : j + chunk] = (hidden * grown).astype(jnp.bfloat16)
        steep = grown + 0.5 * hidden * (1.0 - tangent * tangent) * KAPPA * (1.0 + 3.0 * CUBIC * cell)
        for c in range(width):
            for image in range(images):
                first = (c * images + image) * high
                hidden_grad[first : first + high, j : j + chunk] = (
                    slope[image : image + 1, j : j + chunk] * steep[first : first + high, :]
                ).astype(jnp.bfloat16)
    live = active[...]
    branch_send[...] = jnp.dot(live, down[:, pl.ds(theirs, half)], preferred_element_type=jnp.float32)
    branch_out[...] = jnp.dot(live, down[:, pl.ds(mine, half)], preferred_element_type=jnp.float32)
    back = hidden_grad[...]
    across = (((1,), (1,)), ((), ()))
    grad_y = lax.dot_general(back, up[pl.ds(theirs, half), :], across, preferred_element_type=jnp.float32)
    grad_x = lax.dot_general(back, up[pl.ds(mine, half), :], across, preferred_element_type=jnp.float32)
    grad_send[...] = grad_y.astype(jnp.bfloat16)
    grad_out[...] = grad_x
    gained_x = grad_x * gain_x
    gained_y = grad_y * gain_y
    first_sum = jnp.sum(gained_x, 1, keepdims=True) + jnp.sum(gained_y, 1, keepdims=True)
    second_sum = jnp.sum(gained_x * normed_x, 1, keepdims=True) + jnp.sum(gained_y * normed_y, 1, keepdims=True)
    lane = lax.broadcasted_iota(jnp.int32, (tokens, LANES), 1)
    sums_out[...] = jnp.where(lane == 0, first_sum, second_sum)


def join_kernel(
    branch, branch_other, start, down_bias, layer_scale, grad, grad_other, sums, sums_other, normed, inverse, gain,
    features_out, grad_out, tail_out, head_out, flat, *, rows, width, full
):
    tokens, half = branch.shape
    mine = pl.multiple_of(lax.axis_index("chan") * half, half)
    scale = layer_scale[pl.ds(mine, half)].astype(jnp.float32).reshape(1, half)
    features = start[...] + scale * (branch[...] + branch_other[...] + vec(down_bias))
    for c in range(width):
        for l in range(flat.shape[0]):
            flat[l, pl.ds(c, rows, stride=width), :] = features[
                c * rows : (c + 1) * rows, l * LANES : (l + 1) * LANES
            ]
    for r in range(rows):
        features_out[r] = take(flat, r * width, width, 1).astype(jnp.bfloat16)
    gained = (grad[...] + grad_other[...].astype(jnp.float32)) * vec(gain)
    both = sums[...] + sums_other[...]
    first_sum = both[:, 0:1] / full
    second_sum = both[:, 1:2] / full
    mixed_grad = inverse[:, 0:1] * (gained - first_sum - normed[...] * second_sum)
    grad_out[...] = mixed_grad
    short = mixed_grad.astype(jnp.bfloat16)
    edge = 3 * rows
    tail_out[...] = short[tokens - edge :, :]
    head_out[...] = short[:edge, :]


def unmix_kernel(own, left, right, class_rows, dw_kernel, gradient_out, flat, cols, taps, *, images, high, width):
    rows = images * high
    load_taps(dw_kernel, taps)
    for c in range(3):
        cols[c] = left[c * rows : (c + 1) * rows, :].astype(jnp.float32)
        cols[c + 3 + width] = right[c * rows : (c + 1) * rows, :].astype(jnp.float32)
    for c in range(width):
        cols[c + 3] = own[c * rows : (c + 1) * rows, :]
    classes = class_rows[...]

    def store(c, first, lane, value):
        image = first // high
        flat[lane // LANES, pl.ds(first * width + c, high, stride=width), :] = (
            value + classes[image : image + 1, lane : lane + LANES]
        )

    stencil(cols, taps, store, True, images, high, width)
    for r in range(rows):
        gradient_out[r] = take(flat, r * width, width, 1)


def neighbours(first, second, axis):
    count = lax.axis_size(axis)
    from_left = lax.ppermute(first, axis, [(i, i + 1) for i in range(count - 1)])
    from_right = lax.ppermute(second, axis, [(i + 1, i) for i in range(count - 1)])
    return from_left, from_right


def per_device(
    latents,
    timestep,
    label,
    time_table,
    class_table,
    dw_kernel,
    dw_bias,
    ln_gain,
    ln_bias,
    up_weight,
    up_bias,
    down_weight,
    down_bias,
    layer_scale,
):
    rows, width, half = latents.shape
    full = class_table.shape[1]
    images = timestep.shape[0]
    high = rows // images
    tokens = rows * width
    hidden_size = up_weight.shape[1]
    f32 = jnp.float32
    bf16 = jnp.bfloat16
    sizes = dict(images=images, high=high, width=width)
    swap = [(0, 1), (1, 0)]

    left, right = neighbours(latents, latents, "rows")
    time_rows, class_rows, slope = call(
        functools.partial(setup_kernel, images=images, half=half),
        [((8, half), f32), ((8, half), f32), ((8, hidden_size), f32)],
        [(timestep, pltpu.SMEM), (label, pltpu.SMEM), (time_table, pl.ANY), class_table, layer_scale, down_weight],
        [pltpu.VMEM((images, 8, half), bf16), pltpu.SemaphoreType.DMA((images,))],
        name="setup",
        flops=2 * 96 * full * hidden_size,
    )
    mixed, start = call(
        functools.partial(mix_kernel, **sizes),
        [((tokens + 8, half), f32), ((tokens, half), f32)],
        [latents, left, right, time_rows, dw_kernel, dw_bias, ln_gain, ln_bias],
        [
            pltpu.VMEM((half // LANES, tokens, LANES), f32),
            pltpu.VMEM((width + 6, rows, half), f32),
            pltpu.VMEM((56, half), f32),
        ],
        name="mix",
    )
    mixed_other = lax.ppermute(mixed, "chan", swap)
    branch, branch_send, grad, grad_send, sums, normed, inverse = call(
        functools.partial(mlp_kernel, full=full, chunk=512, **sizes),
        [
            ((tokens, half), f32),
            ((tokens, half), f32),
            ((tokens, half), f32),
            ((tokens, half), bf16),
            ((tokens, LANES), f32),
            ((tokens, half), f32),
            ((tokens, LANES), f32),
        ],
        [mixed, mixed_other, slope, up_weight, up_bias, down_weight],
        [pltpu.VMEM((tokens, hidden_size), bf16), pltpu.VMEM((tokens, hidden_size), bf16)],
        name="mlp",
        limit=40,
    )
    branch_other = lax.ppermute(branch_send, "chan", swap)
    grad_other = lax.ppermute(grad_send, "chan", swap)
    sums_other = lax.ppermute(sums, "chan", swap)
    features, mixed_grad, tail, head = call(
        functools.partial(join_kernel, rows=rows, width=width, full=full),
        [((rows, width, half), bf16), ((tokens, half), f32), ((3 * rows, half), bf16), ((3 * rows, half), bf16)],
        [
            branch, branch_other, start, down_bias, layer_scale,
            grad, grad_other, sums, sums_other, normed, inverse, ln_gain,
        ],
        [pltpu.VMEM((half // LANES, tokens, LANES), f32)],
        name="join",
    )
    features = lax.all_to_all(features, "rows", split_axis=0, concat_axis=1, tiled=True)
    left, right = neighbours(tail, head, "rows")
    (gradient,) = call(
        functools.partial(unmix_kernel, **sizes),
        [((rows, width, half), f32)],
        [mixed_grad, left, right, class_rows, dw_kernel],
        [
            pltpu.VMEM((half // LANES, tokens, LANES), f32),
            pltpu.VMEM((width + 6, rows, half), f32),
            pltpu.VMEM((56, half), f32),
        ],
        name="unmix",
    )
    return features, gradient


def solution(mesh):
    in_specs = (
        P("groups", "rows", "chan"),
        P("groups"),
        P("groups"),
        P(None, "chan"),
        P(),
        P(None, None, "chan"),
        P("chan"),
        P("chan"),
        P("chan"),
        P(None, "chan"),
        P("chan"),
        P("chan", None),
        P("chan"),
        P(),
    )
    out_specs = (P(("groups", "rows"), None, "chan"), P("groups", "rows", "chan"))
    return jax.shard_map(
        per_device, mesh=mesh, in_specs=in_specs, out_specs=out_specs, check_vma=False
    )
```

time: 109 us -> 45.2 us (0.41)
  other arithmetic: 19.8 us -> 0 us
  between operations: 15.5 us -> 0.81 us
  matrix products: 14.5 us -> 0 us
  waiting for transfers between devices: 20.2 us -> 7.51 us
  Pallas kernels: 0 us -> 8.16 us
  blocking collectives: 6.89 us -> 0 us
  starting transfers between devices: 25.1 us -> 19.1 us
  local copies, waits for them, and re-layouts: 5.62 us -> 9.08 us
    dot_general x9 -> x0, matrix products: 14.5 us -> none  [the longest x1 3.82 us: local_block(): jnp.dot(active, down_weight, preferred_element_type=jnp.float32)]
    reduce_scatter x2 -> x0, waiting for transfers between devices: 9.47 us -> none  [the longest x1 9.45 us: local_block(): lax.psum_scatter(grad_terms.astype(jnp.bfloat16), 'chan', scatter_dimensi...]
    pallas_call x0 -> x5, Pallas kernels: none -> 8.16 us  [call(): pl.pallas_call(body, out_shape=tuple((jax.ShapeDtypeStruct(s, d) for s, d...]
    unnamed x166 -> x32, local copies, waits for them, and re-layouts: 0.36 us -> 8.37 us
    convert_element_type x12 -> x0, other arithmetic: 7.82 us -> none  [the longest x1 1.61 us: local_block(): (start_cells + scale_half * branch).astype(jnp.bfloat16)]
    all_to_all x2 -> x1, starting transfers between devices: 13.3 us -> 6.96 us  [per_device(): lax.all_to_all(features, 'rows', split_axis=0, concat_axis=1, tiled=True)]
    all_to_all x2 -> x1, waiting for transfers between devices: 6.28 us -> 0.01 us  [per_device(): lax.all_to_all(features, 'rows', split_axis=0, concat_axis=1, tiled=True)]
    reduce_sum x2 -> x0, other arithmetic: 6.16 us -> none  [the longest x1 5.05 us: local_block(): jnp.sum(flat, 1)]
  transfers between devices with their start and end apart: 8 -> 9, of which waited for: 5 -> 4; matrix products, arithmetic and copies ran while one was open for 23% -> 0% of each run, Pallas kernels for 0% -> 7%
where the time goes in v1:
time: 45.2 us; the launch traced here: 44.7 us
  starting transfers between devices  19.1 us (42%)
  local copies, waits for them, and re-layouts  9.08 us (20%)
  Pallas kernels  8.16 us (18%)
  waiting for transfers between devices  7.51 us (17%)
  between operations  0.81 us (2%)
    ppermute x2, starting transfers between devices, neighbours(): lax.ppermute(first, axis, [(i, i + 1) for i in range(count - 1)])  8.82 us
    unnamed x32, local copies, waits for them, and re-layouts  8.37 us
    pallas_call x5, Pallas kernels, call(): pl.pallas_call(body, out_shape=tuple((jax.ShapeDtypeStruct(s, d) for s, d...  8.16 us
    all_to_all x1, starting transfers between devices, per_device(): lax.all_to_all(features, 'rows', split_axis=0, concat_axis=1, tiled=True)  6.96 us
    ppermute x2, waiting for transfers between devices, neighbours(): lax.ppermute(second, axis, [(i + 1, i) for i in range(count - 1)])  4.29 us
    ppermute x2, starting transfers between devices, neighbours(): lax.ppermute(second, axis, [(i + 1, i) for i in range(count - 1)])  2.58 us
    ppermute x1, waiting for transfers between devices, per_device(): mixed_other = lax.ppermute(mixed, 'chan', swap)  1.45 us
    ppermute x1, waiting for transfers between devices, per_device(): sums_other = lax.ppermute(sums, 'chan', swap)  1.1 us
  transfers between devices with their start and end apart: 9, of which 4 were waited for; matrix products, arithmetic and copies ran while one was open for 0% of the time, Pallas kernels for 7%

profile of v1, /device:TPU:0, one launch (start us, length us, event | category | flops | bytes accessed | tf_op | source)
XLA Modules:
  0.0 44.7 jit_solution(16800908151169855116)
XLA Ops:
  0.6 4.9 %collective-permute-start = (bf16[24,4,512]{2,1,0:T(4,128)(2,1)}, bf16[24,4,512]{2,1,0:T(4,128)(2,1)S(1)}, u32[]{:S(2)}, u32[]{:S(2)}) collective-permute-start(bf16[24,4,512]{2,1,0:T(4,128)(2,1)} %own.1), channel_id=1, source_target_pairs={{0,2},{2,4},{4,6},{6,8},{8,10},{10,12},{12,14},{1,3},{3,5},{5,7},{... | collective-permute-start | bytes 294920 | tf_op jit(solution)/shard_map/ppermute | solution.py:257
  5.5 1.3 %collective-permute-start.1 = (bf16[24,4,512]{2,1,0:T(4,128)(2,1)}, bf16[24,4,512]{2,1,0:T(4,128)(2,1)S(1)}, u32[]{:S(2)}, u32[]{:S(2)}) collective-permute-start(bf16[24,4,512]{2,1,0:T(4,128)(2,1)} %own.1), channel_id=1, source_target_pairs={{2,0},{4,2},{6,4},{8,6},{10,8},{12,10},{14,12},{3,1},{5,3},{7,5},{... | collective-permute-start | bytes 294920 | tf_op jit(solution)/shard_map/ppermute | solution.py:258
  6.9 2.2 %copy-done = bf16[2048,1024]{1,0:T(8,128)(2,1)S(1)} copy-done((bf16[2048,1024]{1,0:T(8,128)(2,1)S(1)}, bf16[2048,1024]{1,0:T(8,128)(2,1)}, u32[]{:S(2)}) %copy-start) | copy-done | bytes 4194328
  9.0 1.2 %copy-done.3 = bf16[1000,512]{1,0:T(8,128)(2,1)S(1)} copy-done((bf16[1000,512]{1,0:T(8,128)(2,1)S(1)}, bf16[1000,512]{1,0:T(8,128)(2,1)}, u32[]{:S(2)}) %copy-start.3) | copy-done | bytes 1024024
  10.3 0.8 %copy-done.6 = bf16[16,1024]{1,0:T(8,128)(2,1)S(1)} copy-done((bf16[16,1024]{1,0:T(8,128)(2,1)S(1)}, bf16[16,1024]{1,0:T(8,128)(2,1)}, u32[]{:S(2)}) %copy-start.6) | copy-done | bytes 32792
  11.0 0.7 %copy-done.7 = bf16[1024]{0:T(1024)(128)(2,1)S(1)} copy-done((bf16[1024]{0:T(1024)(128)(2,1)S(1)}, bf16[1024]{0:T(1024)(128)(2,1)}, u32[]{:S(2)}) %copy-start.7) | copy-done | bytes 2072
  11.7 0.7 %copy-done.14 = s32[3]{0:T(128)S(1)} copy-done((s32[3]{0:T(128)S(1)}, s32[3]{0:T(128)}, u32[]{:S(2)}) %copy-start.14) | copy-done | bytes 36
  12.3 0.7 %copy-done.15 = s32[3]{0:T(128)S(1)} copy-done((s32[3]{0:T(128)S(1)}, s32[3]{0:T(128)}, u32[]{:S(2)}) %copy-start.15) | copy-done | bytes 36
  13.0 1.9 %setup.1 = (f32[8,512]{1,0:T(8,128)S(1)}, f32[8,512]{1,0:T(8,128)S(1)}, f32[8,2048]{1,0:T(8,128)S(1)}) custom-call(s32[3]{0:T(128)S(1)} %copy-done.14, s32[3]{0:T(128)S(1)} %copy-done.15, bf16[1000,512]{1,0:T(8,128)(2,1)S(1)} %copy-done.3, bf16[16,1024]{1,0:T(8,128)(2,1)S(1)} %copy-done.6, bf16[1024]{0:T(1024)(128)(2,1)S(1)} %copy-done.7, ...), custom_call_target="tpu_custom_call" | custom-call | flops 402653184 | tf_op jit(solution)/shard_map/setup/pallas_call | solution.py:24
  15.0 0.8 %mix.1 = (f32[104,512]{1,0:T(8,128)S(1)}, f32[96,512]{1,0:T(8,128)S(1)}) custom-call(bf16[24,4,512]{2,1,0:T(4,128)(2,1)S(1)} %copy-done.5, bf16[24,4,512]{2,1,0:T(4,128)(2,1)S(1)} %collective-permute-done.left, bf16[24,4,512]{2,1,0:T(4,128)(2,1)S(1)} %collective-permute-done.1.right, f32[8,512]{1,0:T(8,128)S(1)} %get-tuple-element.18.time_rows, ...), custom_call_target="tpu_custom_call" | custom-call | tf_op jit(solution)/shard_map/mix/pallas_call | solution.py:24
  15.9 1.5 %collective-permute-done.2.other = f32[104,512]{1,0:T(8,128)S(1)} collective-permute-done((f32[104,512]{1,0:T(8,128)S(1)}, f32[104,512]{1,0:T(8,128)S(1)}, u32[]{:S(2)}, u32[]{:S(2)}) %collective-permute-start.2) | collective-permute-done | bytes 213024 | tf_op jit(solution)/shard_map/ppermute | solution.py:309
  17.4 2.2 %copy-done.2 = bf16[1024,2048]{1,0:T(8,128)(2,1)S(1)} copy-done((bf16[1024,2048]{1,0:T(8,128)(2,1)S(1)}, bf16[1024,2048]{1,0:T(8,128)(2,1)}, u32[]{:S(2)}) %copy-start.2) | copy-done | bytes 4194328
  19.6 3.2 %mlp.1 = (f32[96,512]{1,0:T(8,128)S(1)}, f32[96,512]{1,0:T(8,128)S(1)}, f32[96,512]{1,0:T(8,128)S(1)}, bf16[96,512]{1,0:T(8,128)(2,1)S(1)}, f32[96,128]{1,0:T(8,...) custom-call(f32[104,512]{1,0:T(8,128)S(1)} %get-tuple-element.19.own, ...), custom_call_target="tpu_custom_call" | custom-call | tf_op jit(solution)/shard_map/mlp/pallas_call | solution.py:24
  22.8 0.2 collective-permute-start.3
  23.0 0.4 collective-permute-start.4
  23.5 1.1 %collective-permute-done.5.sums_other = f32[96,128]{1,0:T(8,128)S(1)} collective-permute-done((f32[96,128]{1,0:T(8,128)S(1)}, f32[96,128]{1,0:T(8,128)S(1)}, u32[]{:S(2)}, u32[]{:S(2)}) %collective-permute-start.5) | collective-permute-done | bytes 49184 | tf_op jit(solution)/shard_map/ppermute | solution.py:328
  24.6 0.8 %join.1 = (bf16[24,4,512]{2,1,0:T(4,128)(2,1)}, f32[96,512]{1,0:T(8,128)S(1)}, bf16[72,512]{1,0:T(8,128)(2,1)S(1)}, bf16[72,512]{1,0:T(8,128)(2,1)S(1)}) custom-call(f32[96,512]{1,0:T(8,128)S(1)} %get-tuple-element.21.branch, f32[96,512]{1,0:T(8,128)S(1)} %collective-permute-done.3.branch_other, f32[96,512]{1,0:T(8,128)S(1)} %get-tuple-element.23.start, ...), custom_call_target="tpu_custom_call" | custom-call | tf_op jit(solution)/shard_map/join/pallas_call | solution.py:24
  25.4 7.0 %all-to-all-start = ((bf16[24,4,512]{2,1,0:T(4,128)(2,1)}), bf16[24,4,512]{2,1,0:T(4,128)(2,1)S(1)}, u32[]{:S(2)}, u32[]{:S(2)}) async-start(bf16[24,4,512]{2,1,0:T(4,128)(2,1)} %get-tuple-element.29), calls=%async_computation | async-start | bytes 196608 | tf_op jit(solution)/shard_map/all_to_all | solution.py:339
  32.4 3.9 %collective-permute-start.6 = (bf16[72,512]{1,0:T(8,128)(2,1)S(1)}, bf16[72,512]{1,0:T(8,128)(2,1)S(1)}, u32[]{:S(2)}, u32[]{:S(2)}) collective-permute-start(bf16[72,512]{1,0:T(8,128)(2,1)S(1)} %get-tuple-element.31), channel_id=1, source_target_pairs={{0,2},{2,4},{4,6},{6,8},{8,10},{10,12},{12,14},{1,3},{3,5},{5,7},{... | collective-permute-start | bytes 221192 | tf_op jit(solution)/shard_map/ppermute | solution.py:257
  36.3 1.3 %collective-permute-start.7 = (bf16[72,512]{1,0:T(8,128)(2,1)S(1)}, bf16[72,512]{1,0:T(8,128)(2,1)S(1)}, u32[]{:S(2)}, u32[]{:S(2)}) collective-permute-start(bf16[72,512]{1,0:T(8,128)(2,1)S(1)} %get-tuple-element.32), channel_id=1, source_target_pairs={{2,0},{4,2},{6,4},{8,6},{10,8},{12,10},{14,12},{3,1},{5,3},{7,5},{... | collective-permute-start | bytes 221192 | tf_op jit(solution)/shard_map/ppermute | solution.py:258
  37.6 0.7 %collective-permute-done.6.left = bf16[72,512]{1,0:T(8,128)(2,1)S(1)} collective-permute-done((bf16[72,512]{1,0:T(8,128)(2,1)S(1)}, bf16[72,512]{1,0:T(8,128)(2,1)S(1)}, u32[]{:S(2)}, u32[]{:S(2)}) %collective-permute-start.6) | collective-permute-done | bytes 73760 | tf_op jit(solution)/shard_map/ppermute | solution.py:257
  38.2 4.3 %collective-permute-done.7.right = bf16[72,512]{1,0:T(8,128)(2,1)S(1)} collective-permute-done((bf16[72,512]{1,0:T(8,128)(2,1)S(1)}, bf16[72,512]{1,0:T(8,128)(2,1)S(1)}, u32[]{:S(2)}, u32[]{:S(2)}) %collective-permute-start.7) | collective-permute-done | bytes 73760 | tf_op jit(solution)/shard_map/ppermute | solution.py:258
  42.5 1.5 %unmix.1 = f32[24,4,512]{2,1,0:T(4,128)} custom-call(f32[96,512]{1,0:T(8,128)S(1)} %get-tuple-element.30.own, bf16[72,512]{1,0:T(8,128)(2,1)S(1)} %collective-permute-done.6.left, bf16[72,512]{1,0:T(8,128)(2,1)S(1)} %collective-permute-done.7.right, f32[8,512]{1,0:T(8,128)S(1)} %get-tuple-element.33.class_rows, bf16[7,7,512]{2,1,0:T(8,128)(2,1)S(1)} %copy-done.4), custom_call_target="tpu_custom_call" | custom-call | tf_op jit(solution)/shard_map/unmix/pallas_call | solution.py:24
  44.0 0.7 %all_to_all.16 = bf16[3,32,512]{2,1,0:T(8,128)(2,1)} reshape(bf16[3,8,4,512]{3,2,1,0:T(4,128)(2,1)S(1)} %copy.16) | data formatting | bytes 196608 | tf_op jit(solution)/shard_map/all_to_all | solution.py:339
  (33 shorter events, 0.3 us)
Async XLA Ops:
  0.6 14.3 %collective-permute-start = (bf16[24,4,512]{2,1,0:T(4,128)(2,1)}, bf16[24,4,512]{2,1,0:T(4,128)(2,1)S(1)}, u32[]{:S(2)}, u32[]{:S(2)}) collective-permute-start(bf16[24,4,512]{2,1,0:T(4,128)(2,1)} %own.1), channel_id=1, source_target_pairs={{0,2},{2,4},{4,6},{6,8},{8,10},{10,12},{12,14},{1,3},{3,5},{5,7},{... | collective-permute-start | bytes 294920 | tf_op jit(solution)/shard_map/ppermute | solution.py:257
  5.5 9.4 %collective-permute-start.1 = (bf16[24,4,512]{2,1,0:T(4,128)(2,1)}, bf16[24,4,512]{2,1,0:T(4,128)(2,1)S(1)}, u32[]{:S(2)}, u32[]{:S(2)}) collective-permute-start(bf16[24,4,512]{2,1,0:T(4,128)(2,1)} %own.1), channel_id=1, source_target_pairs={{2,0},{4,2},{6,4},{8,6},{10,8},{12,10},{14,12},{3,1},{5,3},{7,5},{... | collective-permute-start | bytes 294920 | tf_op jit(solution)/shard_map/ppermute | solution.py:258
  6.8 2.2 %copy-start = (bf16[2048,1024]{1,0:T(8,128)(2,1)S(1)}, bf16[2048,1024]{1,0:T(8,128)(2,1)}, u32[]{:S(2)}) copy-start(bf16[2048,1024]{1,0:T(8,128)(2,1)} %down.3) | copy-start | bytes 12582916
  9.0 1.2 %copy-start.3 = (bf16[1000,512]{1,0:T(8,128)(2,1)S(1)}, bf16[1000,512]{1,0:T(8,128)(2,1)}, u32[]{:S(2)}) copy-start(bf16[1000,512]{1,0:T(8,128)(2,1)} %time_table.1) | copy-start | bytes 3072004
  10.3 0.8 %copy-start.6 = (bf16[16,1024]{1,0:T(8,128)(2,1)S(1)}, bf16[16,1024]{1,0:T(8,128)(2,1)}, u32[]{:S(2)}) copy-start(bf16[16,1024]{1,0:T(8,128)(2,1)} %class_table.1) | copy-start | bytes 98308
  11.0 0.7 %copy-start.7 = (bf16[1024]{0:T(1024)(128)(2,1)S(1)}, bf16[1024]{0:T(1024)(128)(2,1)}, u32[]{:S(2)}) copy-start(bf16[1024]{0:T(1024)(128)(2,1)} %layer_scale.3) | copy-start | bytes 6148
  11.7 0.7 %copy-start.14 = (s32[3]{0:T(128)S(1)}, s32[3]{0:T(128)}, u32[]{:S(2)}) copy-start(s32[3]{0:T(128)} %timestep.1) | copy-start | bytes 40
  13.0 2.0 %copy-start.4 = (bf16[7,7,512]{2,1,0:T(8,128)(2,1)S(1)}, bf16[7,7,512]{2,1,0:T(8,128)(2,1)}, u32[]{:S(2)}) copy-start(bf16[7,7,512]{2,1,0:T(8,128)(2,1)} %dw_kernel.3) | copy-start | bytes 150532
  13.0 2.0 %copy-start.5 = (bf16[24,4,512]{2,1,0:T(4,128)(2,1)S(1)}, bf16[24,4,512]{2,1,0:T(4,128)(2,1)}, u32[]{:S(2)}) copy-start(bf16[24,4,512]{2,1,0:T(4,128)(2,1)} %own.1) | copy-start | bytes 294916
  13.0 2.0 %copy-start.10 = (bf16[512]{0:T(512)(128)(2,1)S(1)}, bf16[512]{0:T(512)(128)(2,1)}, u32[]{:S(2)}) copy-start(bf16[512]{0:T(512)(128)(2,1)} %gain.3) | copy-start | bytes 3076
  13.0 2.0 %copy-start.11 = (bf16[512]{0:T(512)(128)(2,1)S(1)}, bf16[512]{0:T(512)(128)(2,1)}, u32[]{:S(2)}) copy-start(bf16[512]{0:T(512)(128)(2,1)} %dw_bias.1) | copy-start | bytes 3076
  13.0 2.0 %copy-start.12 = (bf16[512]{0:T(512)(128)(2,1)S(1)}, bf16[512]{0:T(512)(128)(2,1)}, u32[]{:S(2)}) copy-start(bf16[512]{0:T(512)(128)(2,1)} %shift.1) | copy-start | bytes 3076
  13.0 4.4 %copy-start.1 = (bf16[2048,1024]{1,0:T(8,128)(2,1)S(1)}, bf16[2048,1024]{1,0:T(8,128)(2,1)}, u32[]{:S(2)}) copy-start(bf16[2048,1024]{1,0:T(8,128)(2,1)} %down.3) | copy-start | bytes 12582916
  13.0 4.4 %copy-start.9 = (bf16[2048]{0:T(1024)(128)(2,1)S(1)}, bf16[2048]{0:T(1024)(128)(2,1)}, u32[]{:S(2)}) copy-start(bf16[2048]{0:T(1024)(128)(2,1)} %up_bias.1) | copy-start | bytes 12292
  15.9 1.5 %collective-permute-start.2 = (f32[104,512]{1,0:T(8,128)S(1)}, f32[104,512]{1,0:T(8,128)S(1)}, u32[]{:S(2)}, u32[]{:S(2)}) collective-permute-start(f32[104,512]{1,0:T(8,128)S(1)} %get-tuple-element.19.own), channel_id=1, source_target_pairs={{0,1},{1,0},{2,3},{3,2},{4,5},{5,4},{6,7},{7,6},{8,9},{9,8},{10,11... | collective-permute-start | bytes 638984 | tf_op jit(solution)/shard_map/ppermute | solution.py:309
  17.4 2.2 %copy-start.2 = (bf16[1024,2048]{1,0:T(8,128)(2,1)S(1)}, bf16[1024,2048]{1,0:T(8,128)(2,1)}, u32[]{:S(2)}) copy-start(bf16[1024,2048]{1,0:T(8,128)(2,1)} %up.1) | copy-start | bytes 12582916
  19.6 5.0 %copy-start.8 = (bf16[1024]{0:T(1024)(128)(2,1)S(1)}, bf16[1024]{0:T(1024)(128)(2,1)}, u32[]{:S(2)}) copy-start(bf16[1024]{0:T(1024)(128)(2,1)} %layer_scale.3) | copy-start | bytes 6148
  19.6 5.0 %copy-start.13 = (bf16[512]{0:T(512)(128)(2,1)S(1)}, bf16[512]{0:T(512)(128)(2,1)}, u32[]{:S(2)}) copy-start(bf16[512]{0:T(512)(128)(2,1)} %down_bias.1) | copy-start | bytes 3076
  22.8 1.8 %collective-permute-start.3 = (f32[96,512]{1,0:T(8,128)S(1)}, f32[96,512]{1,0:T(8,128)S(1)}, u32[]{:S(2)}, u32[]{:S(2)}) collective-permute-start(f32[96,512]{1,0:T(8,128)S(1)} %get-tuple-element.22), channel_id=1, source_target_pairs={{0,1},{1,0},{2,3},{3,2},{4,5},{5,4},{6,7},{7,6},{8,9},{9,8},{10,11... | collective-permute-start | bytes 589832 | tf_op jit(solution)/shard_map/ppermute | solution.py:326
  23.0 1.6 %collective-permute-start.4 = (bf16[96,512]{1,0:T(8,128)(2,1)S(1)}, bf16[96,512]{1,0:T(8,128)(2,1)S(1)}, u32[]{:S(2)}, u32[]{:S(2)}) collective-permute-start(bf16[96,512]{1,0:T(8,128)(2,1)S(1)} %get-tuple-element.25), channel_id=1, source_target_pairs={{0,1},{1,0},{2,3},{3,2},{4,5},{5,4},{6,7},{7,6},{8,9},{9,8},{10,11... | collective-permute-start | bytes 294920 | tf_op jit(solution)/shard_map/ppermute | solution.py:327
  23.3 1.2 %collective-permute-start.5 = (f32[96,128]{1,0:T(8,128)S(1)}, f32[96,128]{1,0:T(8,128)S(1)}, u32[]{:S(2)}, u32[]{:S(2)}) collective-permute-start(f32[96,128]{1,0:T(8,128)S(1)} %get-tuple-element.26.sums), channel_id=1, source_target_pairs={{0,1},{1,0},{2,3},{3,2},{4,5},{5,4},{6,7},{7,6},{8,9},{9,8},{10,11... | collective-permute-start | bytes 147464 | tf_op jit(solution)/shard_map/ppermute | solution.py:328
  25.4 18.6 %all-to-all-start = ((bf16[24,4,512]{2,1,0:T(4,128)(2,1)}), bf16[24,4,512]{2,1,0:T(4,128)(2,1)S(1)}, u32[]{:S(2)}, u32[]{:S(2)}) async-start(bf16[24,4,512]{2,1,0:T(4,128)(2,1)} %get-tuple-element.29), calls=%async_computation | async-start | bytes 196608 | tf_op jit(solution)/shard_map/all_to_all | solution.py:339
  32.4 5.9 %collective-permute-start.6 = (bf16[72,512]{1,0:T(8,128)(2,1)S(1)}, bf16[72,512]{1,0:T(8,128)(2,1)S(1)}, u32[]{:S(2)}, u32[]{:S(2)}) collective-permute-start(bf16[72,512]{1,0:T(8,128)(2,1)S(1)} %get-tuple-element.31), channel_id=1, source_target_pairs={{0,2},{2,4},{4,6},{6,8},{8,10},{10,12},{12,14},{1,3},{3,5},{5,7},{... | collective-permute-start | bytes 221192 | tf_op jit(solution)/shard_map/ppermute | solution.py:257
  36.3 6.2 %collective-permute-start.7 = (bf16[72,512]{1,0:T(8,128)(2,1)S(1)}, bf16[72,512]{1,0:T(8,128)(2,1)S(1)}, u32[]{:S(2)}, u32[]{:S(2)}) collective-permute-start(bf16[72,512]{1,0:T(8,128)(2,1)S(1)} %get-tuple-element.32), channel_id=1, source_target_pairs={{2,0},{4,2},{6,4},{8,6},{10,8},{12,10},{14,12},{3,1},{5,3},{7,5},{... | collective-permute-start | bytes 221192 | tf_op jit(solution)/shard_map/ppermute | solution.py:258
  (1 other events, 0.7 us)

commit v2 on v1

--- a/solution.py
+++ b/solution.py
@@ -14,12 +14,14 @@
 MIB = 1 << 20
 
 
-def call(body, outs, ins, scratch=(), limit=24, name=None, flops=0):
+def call(body, outs, ins, scratch=(), limit=16, name=None, flops=0):
     specs = []
     args = []
     for item in ins:
         array, space = item if isinstance(item, tuple) else (item, pltpu.VMEM)
         specs.append(pl.BlockSpec(memory_space=space))
+        if space == pltpu.HBM:
+            array = pltpu.with_memory_space_constraint(array, pltpu.HBM)
         args.append(array)
     return pl.pallas_call(
         body,
@@ -48,31 +50,37 @@
 
 
 def setup_kernel(
-    timestep, label, time_table, class_table, layer_scale, down, time_out, class_out, slope_out, rows8, sems,
-    *, images, half
-):
-    copies = []
+    timestep, label, time_table, class_table, layer_scale, down, time_out, class_out, slope_out, down_out,
+    step, kind, table, scale, rows8, sems, *, images, half
+):
+    pairs = ((timestep, step), (label, kind), (class_table, table), (layer_scale, scale), (down, down_out))
+    copies = [pltpu.make_async_copy(a, b, sems.at[i]) for i, (a, b) in enumerate(pairs)]
+    for copy in copies:
+        copy.start()
+    copies[0].wait()
     for i in range(images):
-        base = pl.multiple_of((timestep[i] // 8) * 8, 8)
+        base = pl.multiple_of((step[i] // 8) * 8, 8)
         copies.append(
-            pltpu.make_async_copy(time_table.at[pl.ds(base, 8), :], rows8.at[i], sems.at[i])
+            pltpu.make_async_copy(time_table.at[pl.ds(base, 8), :], rows8.at[i], sems.at[len(pairs) + i])
         )
         copies[-1].start()
+    for copy in copies[1:4]:
+        copy.wait()
     mine = pl.multiple_of(lax.axis_index("chan") * half, half)
-    scale = vec(layer_scale)
-    table = class_table[...].astype(jnp.float32)
-    table_half = class_table[:, pl.ds(mine, half)].astype(jnp.float32)
-    full = [row_of(table, label[i]) for i in range(images)]
+    whole = table[...].astype(jnp.float32)
+    part = table[:, pl.ds(mine, half)].astype(jnp.float32)
+    full = [row_of(whole, kind[i]) for i in range(images)]
     for i in range(images):
-        class_out[i : i + 1, :] = row_of(table_half, label[i])
+        class_out[i : i + 1, :] = row_of(part, kind[i])
     fill = [jnp.zeros_like(full[0])] * (8 - images)
-    direction = (jnp.concatenate(full + fill, axis=0) * scale).astype(jnp.bfloat16)
+    direction = (jnp.concatenate(full + fill, axis=0) * vec(scale)).astype(jnp.bfloat16)
+    for i in range(images):
+        copies[len(pairs) + i].wait()
+        time_out[i : i + 1, :] = row_of(rows8[i].astype(jnp.float32), step[i] % 8)
+    copies[4].wait()
     slope_out[...] = lax.dot_general(
-        direction, down[...], (((1,), (1,)), ((), ())), preferred_element_type=jnp.float32
-    )
-    for i in range(images):
-        copies[i].wait()
-        time_out[i : i + 1, :] = row_of(rows8[i].astype(jnp.float32), timestep[i] % 8)
+        direction, down_out[...], (((1,), (1,)), ((), ())), preferred_element_type=jnp.float32
+    )
 
 
 def stencil(cols, taps, store, flip, images, high, width):
@@ -146,9 +154,9 @@
     mixed_out[tokens + 1 : tokens + 2, :] = vec(shift)
 
 
-def mlp_kernel(
-    own, other, slope, up, up_bias, down, branch_out, branch_send, grad_out, grad_send, sums_out, normed_out, inverse_out,
-    active, hidden_grad, *, images, high, width, full, chunk
+def forward_kernel(
+    own, other, slope, up, up_bias, down, branch_out, branch_send, hidden_grad, normed_out, normed_other_out, inverse_out,
+    active, *, images, high, width, full, chunk
 ):
     tokens = images * high * width
     half = own.shape[1]
@@ -163,11 +171,12 @@
     inverse = lax.rsqrt(square - mean * mean + EPSILON)
     normed_x = (x - mean) * inverse
     normed_y = (y - mean) * inverse
-    gain_x = own[tokens : tokens + 1, :]
-    gain_y = other[tokens : tokens + 1, :]
-    scaled_x = (normed_x * gain_x + own[tokens + 1 : tokens + 2, :]).astype(jnp.bfloat16)
-    scaled_y = (normed_y * gain_y + other[tokens + 1 : tokens + 2, :]).astype(jnp.bfloat16)
+    scaled_x = normed_x * own[tokens : tokens + 1, :] + own[tokens + 1 : tokens + 2, :]
+    scaled_y = normed_y * other[tokens : tokens + 1, :] + other[tokens + 1 : tokens + 2, :]
+    scaled_x = scaled_x.astype(jnp.bfloat16)
+    scaled_y = scaled_y.astype(jnp.bfloat16)
     normed_out[...] = normed_x
+    normed_other_out[...] = normed_y
     inverse_out[...] = jnp.broadcast_to(inverse, inverse_out.shape)
     bias = vec(up_bias)
     for j in range(0, hidden_size, chunk):
@@ -190,24 +199,33 @@
     live = active[...]
     branch_send[...] = jnp.dot(live, down[:, pl.ds(theirs, half)], preferred_element_type=jnp.float32)
     branch_out[...] = jnp.dot(live, down[:, pl.ds(mine, half)], preferred_element_type=jnp.float32)
+
+
+def backward_kernel(
+    hidden_grad, up, own, other, normed, normed_other, grad_out, grad_send, sums_out
+):
+    tokens, half = normed.shape
+    index = lax.axis_index("chan")
+    mine = pl.multiple_of(index * half, half)
+    theirs = pl.multiple_of((1 - index) * half, half)
     back = hidden_grad[...]
     across = (((1,), (1,)), ((), ()))
     grad_y = lax.dot_general(back, up[pl.ds(theirs, half), :], across, preferred_element_type=jnp.float32)
     grad_x = lax.dot_general(back, up[pl.ds(mine, half), :], across, preferred_element_type=jnp.float32)
-    grad_send[...] = grad_y.astype(jnp.bfloat16)
+    grad_send[:, :half] = grad_y.astype(jnp.bfloat16)
     grad_out[...] = grad_x
-    gained_x = grad_x * gain_x
-    gained_y = grad_y * gain_y
-    first_sum = jnp.sum(gained_x, 1, keepdims=True) + jnp.sum(gained_y, 1, keepdims=True)
-    second_sum = jnp.sum(gained_x * normed_x, 1, keepdims=True) + jnp.sum(gained_y * normed_y, 1, keepdims=True)
+    gained_x = grad_x * own[tokens : tokens + 1, :]
+    gained_y = grad_y * other[tokens : tokens + 1, :]
+    first_sum = jnp.sum(gained_x + gained_y, 1, keepdims=True)
+    second_sum = jnp.sum(gained_x * normed[...] + gained_y * normed_other[...], 1, keepdims=True)
     lane = lax.broadcasted_iota(jnp.int32, (tokens, LANES), 1)
-    sums_out[...] = jnp.where(lane == 0, first_sum, second_sum)
-
-
-def join_kernel(
-    branch, branch_other, start, down_bias, layer_scale, grad, grad_other, sums, sums_other, normed, inverse, gain,
-    features_out, grad_out, tail_out, head_out, flat, *, rows, width, full
-):
+    sums = jnp.where(lane % 2 == 0, first_sum, second_sum)
+    sums_out[...] = sums
+    coarse = sums.astype(jnp.bfloat16).astype(jnp.float32)
+    grad_send[:, half:] = jnp.where(lane < 2, coarse, sums - coarse).astype(jnp.bfloat16)
+
+
+def features_kernel(branch, branch_other, start, down_bias, layer_scale, features_out, flat, *, rows, width):
     tokens, half = branch.shape
     mine = pl.multiple_of(lax.axis_index("chan") * half, half)
     scale = layer_scale[pl.ds(mine, half)].astype(jnp.float32).reshape(1, half)
@@ -219,24 +237,36 @@
             ]
     for r in range(rows):
         features_out[r] = take(flat, r * width, width, 1).astype(jnp.bfloat16)
-    gained = (grad[...] + grad_other[...].astype(jnp.float32)) * vec(gain)
-    both = sums[...] + sums_other[...]
-    first_sum = both[:, 0:1] / full
-    second_sum = both[:, 1:2] / full
-    mixed_grad = inverse[:, 0:1] * (gained - first_sum - normed[...] * second_sum)
-    grad_out[...] = mixed_grad
-    short = mixed_grad.astype(jnp.bfloat16)
+
+
+def norm_grad_kernel(
+    grad, grad_other, sums, normed, inverse, gain, grad_out, inner_out, outer_out, *, rows, full
+):
+    tokens, half = grad.shape
+    gained = (grad[...] + grad_other[:, :half].astype(jnp.float32)) * vec(gain)
+    extra = grad_other[:, half:].astype(jnp.float32)
+    first_sum = (sums[:, 0:1] + (extra[:, 0:1] + extra[:, 2:3])) / full
+    second_sum = (sums[:, 1:2] + (extra[:, 1:2] + extra[:, 3:4])) / full
+    grad_out[...] = inverse[:, 0:1] * (gained - first_sum - normed[...] * second_sum)
     edge = 3 * rows
-    tail_out[...] = short[tokens - edge :, :]
-    head_out[...] = short[:edge, :]
-
-
-def unmix_kernel(own, left, right, class_rows, dw_kernel, gradient_out, flat, cols, taps, *, images, high, width):
+    parity = lax.axis_index("rows") % 2
+    low = pl.multiple_of(parity * (tokens - edge), 8)
+    high = pl.multiple_of((1 - parity) * (tokens - edge), 8)
+    inner_out[...] = grad_out[pl.ds(high, edge), :].astype(jnp.bfloat16)
+    outer_out[...] = grad_out[pl.ds(low, edge), :].astype(jnp.bfloat16)
+
+
+def unmix_kernel(own, inner, outer, class_rows, dw_kernel, gradient_out, flat, cols, taps, *, images, high, width):
     rows = images * high
     load_taps(dw_kernel, taps)
+    position = lax.axis_index("rows")
+    parity = position % 2
+    within = (position > 0) & (position < lax.axis_size("rows") - 1)
+    inner_side = pl.multiple_of((1 - parity) * (3 + width), 1)
+    outer_side = pl.multiple_of(parity * (3 + width), 1)
     for c in range(3):
-        cols[c] = left[c * rows : (c + 1) * rows, :].astype(jnp.float32)
-        cols[c + 3 + width] = right[c * rows : (c + 1) * rows, :].astype(jnp.float32)
+        cols[inner_side + c] = inner[c * rows : (c + 1) * rows, :].astype(jnp.float32)
+        cols[outer_side + c] = outer[c * rows : (c + 1) * rows, :].astype(jnp.float32) * jnp.where(within, 1.0, 0.0)
     for c in range(width):
         cols[c + 3] = own[c * rows : (c + 1) * rows, :]
     classes = class_rows[...]
@@ -287,11 +317,18 @@
     swap = [(0, 1), (1, 0)]
 
     left, right = neighbours(latents, latents, "rows")
-    time_rows, class_rows, slope = call(
+    time_rows, class_rows, slope, down = call(
         functools.partial(setup_kernel, images=images, half=half),
-        [((8, half), f32), ((8, half), f32), ((8, hidden_size), f32)],
-        [(timestep, pltpu.SMEM), (label, pltpu.SMEM), (time_table, pl.ANY), class_table, layer_scale, down_weight],
-        [pltpu.VMEM((images, 8, half), bf16), pltpu.SemaphoreType.DMA((images,))],
+        [((8, half), f32), ((8, half), f32), ((8, hidden_size), f32), (down_weight.shape, bf16)],
+        [(a, pltpu.HBM) for a in (timestep, label, time_table, class_table, layer_scale, down_weight)],
+        [
+            pltpu.SMEM(timestep.shape, jnp.int32),
+            pltpu.SMEM(label.shape, jnp.int32),
+            pltpu.VMEM(class_table.shape, bf16),
+            pltpu.VMEM(layer_scale.shape, bf16),
+            pltpu.VMEM((images, 8, half), bf16),
+            pltpu.SemaphoreType.DMA((5 + images,)),
+        ],
         name="setup",
         flops=2 * 96 * full * hidden_size,
     )
@@ -307,41 +344,49 @@
         name="mix",
     )
     mixed_other = lax.ppermute(mixed, "chan", swap)
-    branch, branch_send, grad, grad_send, sums, normed, inverse = call(
-        functools.partial(mlp_kernel, full=full, chunk=512, **sizes),
+    branch, branch_send, hidden_grad, normed, normed_other, inverse = call(
+        functools.partial(forward_kernel, full=full, chunk=512, **sizes),
         [
             ((tokens, half), f32),
             ((tokens, half), f32),
+            ((tokens, hidden_size), bf16),
             ((tokens, half), f32),
-            ((tokens, half), bf16),
-            ((tokens, LANES), f32),
             ((tokens, half), f32),
             ((tokens, LANES), f32),
         ],
-        [mixed, mixed_other, slope, up_weight, up_bias, down_weight],
-        [pltpu.VMEM((tokens, hidden_size), bf16), pltpu.VMEM((tokens, hidden_size), bf16)],
-        name="mlp",
-        limit=40,
+        [mixed, mixed_other, slope, up_weight, up_bias, down],
+        [pltpu.VMEM((tokens, hidden_size), bf16)],
+        name="forward",
     )
     branch_other = lax.ppermute(branch_send, "chan", swap)
+    grad, grad_send, sums = call(
+        backward_kernel,
+        [((tokens, half), f32), ((tokens, half + LANES), bf16), ((tokens, LANES), f32)],
+        [hidden_grad, up_weight, mixed, mixed_other, normed, normed_other],
+        name="backward",
+    )
     grad_other = lax.ppermute(grad_send, "chan", swap)
-    sums_other = lax.ppermute(sums, "chan", swap)
-    features, mixed_grad, tail, head = call(
-        functools.partial(join_kernel, rows=rows, width=width, full=full),
-        [((rows, width, half), bf16), ((tokens, half), f32), ((3 * rows, half), bf16), ((3 * rows, half), bf16)],
-        [
-            branch, branch_other, start, down_bias, layer_scale,
-            grad, grad_other, sums, sums_other, normed, inverse, ln_gain,
-        ],
+    (features,) = call(
+        functools.partial(features_kernel, rows=rows, width=width),
+        [((rows, width, half), bf16)],
+        [branch, branch_other, start, down_bias, layer_scale],
         [pltpu.VMEM((half // LANES, tokens, LANES), f32)],
         name="join",
     )
     features = lax.all_to_all(features, "rows", split_axis=0, concat_axis=1, tiled=True)
-    left, right = neighbours(tail, head, "rows")
+    mixed_grad, inner, outer = call(
+        functools.partial(norm_grad_kernel, rows=rows, full=full),
+        [((tokens, half), f32), ((3 * rows, half), bf16), ((3 * rows, half), bf16)],
+        [grad, grad_other, sums, normed, inverse, ln_gain],
+        name="norm_grad",
+    )
+    count = lax.axis_size("rows")
+    inner = lax.ppermute(inner, "rows", [(i, i ^ 1) for i in range(count)])
+    outer = lax.ppermute(outer, "rows", [(i, min(max((i + 1 ^ 1) - 1, 0), count - 1)) for i in range(count)])
     (gradient,) = call(
         functools.partial(unmix_kernel, **sizes),
         [((rows, width, half), f32)],
-        [mixed_grad, left, right, class_rows, dw_kernel],
+        [mixed_grad, inner, outer, class_rows, dw_kernel],
         [
             pltpu.VMEM((half // LANES, tokens, LANES), f32),
             pltpu.VMEM((width + 6, rows, half), f32),

time: 45.2 us -> 36 us (0.80)
  the two profiles are of different devices: /device:TPU:0 before, /device:TPU:8 now
where the time goes in v2:
time: 36 us; the launch traced here: 35.6 us
  starting transfers between devices  17.2 us (48%)
  Pallas kernels  10.2 us (28%)
  waiting for transfers between devices  6.67 us (19%)
  between operations  0.83 us (2%)
  local copies, waits for them, and re-layouts  0.75 us (2%)
    pallas_call x7, Pallas kernels, call(): pl.pallas_call(body, out_shape=tuple((jax.ShapeDtypeStruct(s, d) for s, d...  10.2 us
    all_to_all x1, starting transfers between devices, per_device(): lax.all_to_all(features, 'rows', split_axis=0, concat_axis=1, tiled=True)  6.02 us
    ppermute x1, waiting for transfers between devices, per_device(): lax.ppermute(outer, 'rows', [(i, min(max((i + 1 ^ 1) - 1, 0), count - 1))...  4.08 us
    ppermute x1, starting transfers between devices, neighbours(): lax.ppermute(first, axis, [(i, i + 1) for i in range(count - 1)])  3.69 us
    ppermute x1, starting transfers between devices, neighbours(): lax.ppermute(second, axis, [(i + 1, i) for i in range(count - 1)])  3.31 us
    ppermute x1, starting transfers between devices, per_device(): lax.ppermute(outer, 'rows', [(i, min(max((i + 1 ^ 1) - 1, 0), count - 1))...  1.92 us
    ppermute x1, starting transfers between devices, per_device(): inner = lax.ppermute(inner, 'rows', [(i, i ^ 1) for i in range(count)])  1.53 us
    ppermute x1, waiting for transfers between devices, per_device(): mixed_other = lax.ppermute(mixed, 'chan', swap)  1.45 us
  transfers between devices with their start and end apart: 8, of which 3 were waited for; matrix products, arithmetic and copies ran while one was open for 0% of the time, Pallas kernels for 21%

profile of v2, /device:TPU:8, one launch (start us, length us, event | category | flops | bytes accessed | tf_op | source)
XLA Modules:
  0.0 35.6 jit_solution(1065041256951000600)
XLA Ops:
  0.7 3.7 %collective-permute-start = (bf16[24,4,512]{2,1,0:T(4,128)(2,1)}, bf16[24,4,512]{2,1,0:T(4,128)(2,1)S(1)}, u32[]{:S(2)}, u32[]{:S(2)}) collective-permute-start(bf16[24,4,512]{2,1,0:T(4,128)(2,1)} %own.1), channel_id=1, source_target_pairs={{0,2},{2,4},{4,6},{6,8},{8,10},{10,12},{12,14},{1,3},{3,5},{5,7},{... | collective-permute-start | bytes 294920 | tf_op jit(solution)/shard_map/ppermute | solution.py:287
  4.4 3.3 %collective-permute-start.1 = (bf16[24,4,512]{2,1,0:T(4,128)(2,1)}, bf16[24,4,512]{2,1,0:T(4,128)(2,1)S(1)}, u32[]{:S(2)}, u32[]{:S(2)}) collective-permute-start(bf16[24,4,512]{2,1,0:T(4,128)(2,1)} %own.1), channel_id=1, source_target_pairs={{2,0},{4,2},{6,4},{8,6},{10,8},{12,10},{14,12},{3,1},{5,3},{7,5},{... | collective-permute-start | bytes 294920 | tf_op jit(solution)/shard_map/ppermute | solution.py:288
  7.7 3.5 %setup.1 = (f32[8,512]{1,0:T(8,128)S(1)}, f32[8,512]{1,0:T(8,128)S(1)}, f32[8,2048]{1,0:T(8,128)S(1)}, bf16[2048,1024]{1,0:T(8,128)(2,1)S(1)}) custom-call(s32[3]{0:T(128)} %timestep.1, s32[3]{0:T(128)} %label.1, bf16[1000,512]{1,0:T(8,128)(2,1)} %time_table.1, bf16[16,1024]{1,0:T(8,128)(2,1)} %class_table.1, bf16[1024]{0:T(1024)(128)(2,1)} %layer_scale.3, ...), custom_call_target="tpu_custom_call" | custom-call | flops 402653184 | tf_op jit(solution)/shard_map/setup/pallas_call | solution.py:26
  11.2 0.0 collective-permute-done.left
  11.3 0.8 %mix.1 = (f32[104,512]{1,0:T(8,128)S(1)}, f32[96,512]{1,0:T(8,128)S(1)}) custom-call(bf16[24,4,512]{2,1,0:T(4,128)(2,1)S(1)} %copy-done.2, bf16[24,4,512]{2,1,0:T(4,128)(2,1)S(1)} %collective-permute-done.left, bf16[24,4,512]{2,1,0:T(4,128)(2,1)S(1)} %collective-permute-done.1.right, f32[8,512]{1,0:T(8,128)S(1)} %get-tuple-element.20.time_rows, ...), custom_call_target="tpu_custom_call" | custom-call | tf_op jit(solution)/shard_map/mix/pallas_call | solution.py:26
  12.1 0.1 collective-permute-start.2
  12.2 1.5 %collective-permute-done.2.other = f32[104,512]{1,0:T(8,128)S(1)} collective-permute-done((f32[104,512]{1,0:T(8,128)S(1)}, f32[104,512]{1,0:T(8,128)S(1)}, u32[]{:S(2)}, u32[]{:S(2)}) %collective-permute-start.2) | collective-permute-done | bytes 213024 | tf_op jit(solution)/shard_map/ppermute | solution.py:346
  13.7 2.0 %forward.1 = (f32[96,512]{1,0:T(8,128)S(1)}, f32[96,512]{1,0:T(8,128)S(1)}, bf16[96,2048]{1,0:T(8,128)(2,1)S(1)}, f32[96,512]{1,0:T(8,128)S(1)}, f32[96,512]{1,0:T(8,128)S(1)}, /*index=5*/f32[96,128]{1,0:T(8,128)S(1)}) custom-call(f32[104,512]{1,0:T(8,128)S(1)} %get-tuple-element.21.own, f32[104,512]{1,0:T(8,128)S(1)} %collective-permute-done.2.other, ...), custom_call_target="tpu_custom_call" | custom-call | tf_op jit(solution)/shard_map/forward/pallas_call | solution.py:26
  15.6 0.0 copy-start.3
  15.7 0.0 copy-start.8
  15.7 0.2 collective-permute-start.3
  15.8 1.5 %backward.1 = (f32[96,512]{1,0:T(8,128)S(1)}, bf16[96,640]{1,0:T(8,128)(2,1)S(1)}, f32[96,128]{1,0:T(8,128)S(1)}) custom-call(bf16[96,2048]{1,0:T(8,128)(2,1)S(1)} %get-tuple-element.27.hidden_grad, bf16[1024,2048]{1,0:T(8,128)(2,1)S(1)} %copy-done, f32[104,512]{1,0:T(8,128)S(1)} %get-tuple-element.21.own, f32[104,512]{1,0:T(8,128)S(1)} %collective-permute-done.2.other, ...), custom_call_target="tpu_custom_call" | custom-call | tf_op jit(solution)/shard_map/backward/pallas_call | solution.py:26
  17.3 0.5 %collective-permute-start.4 = (bf16[96,640]{1,0:T(8,128)(2,1)S(1)}, bf16[96,640]{1,0:T(8,128)(2,1)S(1)}, u32[]{:S(2)}, u32[]{:S(2)}) collective-permute-start(bf16[96,640]{1,0:T(8,128)(2,1)S(1)} %get-tuple-element.31), channel_id=1, source_target_pairs={{0,1},{1,0},{2,3},{3,2},{4,5},{5,4},{6,7},{7,6},{8,9},{9,8},{10,11... | collective-permute-start | bytes 368648 | tf_op jit(solution)/shard_map/ppermute | solution.py:368
  17.8 0.0 collective-permute-done.3.branch_other
  17.8 0.7 %join.1 = bf16[24,4,512]{2,1,0:T(4,128)(2,1)} custom-call(f32[96,512]{1,0:T(8,128)S(1)} %get-tuple-element.24.branch, f32[96,512]{1,0:T(8,128)S(1)} %collective-permute-done.3.branch_other, f32[96,512]{1,0:T(8,128)S(1)} %get-tuple-element.26.start, bf16[512]{0:T(512)(128)(2,1)S(1)} %copy-done.8, bf16[1024]{0:T(1024)(128)(2,1)S(1)} %copy-done.3), custom_call_target="tpu_custom_call" | custom-call | tf_op jit(solution)/shard_map/join/pallas_call | solution.py:26
  18.6 6.0 %all-to-all-start = ((bf16[24,4,512]{2,1,0:T(4,128)(2,1)}), bf16[24,4,512]{2,1,0:T(4,128)(2,1)S(1)}, u32[]{:S(2)}, u32[]{:S(2)}) async-start(bf16[24,4,512]{2,1,0:T(4,128)(2,1)} %join.1), calls=%async_computation | async-start | bytes 196608 | tf_op jit(solution)/shard_map/all_to_all | solution.py:376
  24.6 0.0 collective-permute-done.4.grad_other
  24.6 0.2 norm_grad.1
  24.8 1.5 %collective-permute-start.5 = (bf16[72,512]{1,0:T(8,128)(2,1)S(1)}, bf16[72,512]{1,0:T(8,128)(2,1)S(1)}, u32[]{:S(2)}, u32[]{:S(2)}) collective-permute-start(bf16[72,512]{1,0:T(8,128)(2,1)S(1)} %get-tuple-element.35), channel_id=1, source_target_pairs={{0,2},{2,0},{4,6},{6,4},{8,10},{10,8},{12,14},{14,12},{1,3},{3,1},... | collective-permute-start | bytes 221192 | tf_op jit(solution)/shard_map/ppermute | solution.py:384
  26.3 1.9 %collective-permute-start.6 = (bf16[72,512]{1,0:T(8,128)(2,1)S(1)}, bf16[72,512]{1,0:T(8,128)(2,1)S(1)}, u32[]{:S(2)}, u32[]{:S(2)}) collective-permute-start(bf16[72,512]{1,0:T(8,128)(2,1)S(1)} %get-tuple-element.36), channel_id=1, source_target_pairs={{0,0},{2,4},{4,2},{6,8},{8,6},{10,12},{12,10},{14,14},{1,1},{3,5},... | collective-permute-start | bytes 221192 | tf_op jit(solution)/shard_map/ppermute | solution.py:385
  28.2 1.1 %collective-permute-done.5.inner = bf16[72,512]{1,0:T(8,128)(2,1)S(1)} collective-permute-done((bf16[72,512]{1,0:T(8,128)(2,1)S(1)}, bf16[72,512]{1,0:T(8,128)(2,1)S(1)}, u32[]{:S(2)}, u32[]{:S(2)}) %collective-permute-start.5) | collective-permute-done | bytes 73760 | tf_op jit(solution)/shard_map/ppermute | solution.py:384
  29.4 4.1 %collective-permute-done.6.outer = bf16[72,512]{1,0:T(8,128)(2,1)S(1)} collective-permute-done((bf16[72,512]{1,0:T(8,128)(2,1)S(1)}, bf16[72,512]{1,0:T(8,128)(2,1)S(1)}, u32[]{:S(2)}, u32[]{:S(2)}) %collective-permute-start.6) | collective-permute-done | bytes 73760 | tf_op jit(solution)/shard_map/ppermute | solution.py:385
  33.4 1.5 %unmix.1 = f32[24,4,512]{2,1,0:T(4,128)} custom-call(f32[96,512]{1,0:T(8,128)S(1)} %get-tuple-element.34.own, bf16[72,512]{1,0:T(8,128)(2,1)S(1)} %collective-permute-done.5.inner, bf16[72,512]{1,0:T(8,128)(2,1)S(1)} %collective-permute-done.6.outer, f32[8,512]{1,0:T(8,128)S(1)} %get-tuple-element.37.class_rows, bf16[7,7,512]{2,1,0:T(8,128)(2,1)S(1)} %copy-done.1), custom_call_target="tpu_custom_call" | custom-call | tf_op jit(solution)/shard_map/unmix/pallas_call | solution.py:26
  35.0 0.7 %all_to_all.16 = bf16[3,32,512]{2,1,0:T(8,128)(2,1)} reshape(bf16[3,8,4,512]{3,2,1,0:T(4,128)(2,1)S(1)} %copy.16) | data formatting | bytes 196608 | tf_op jit(solution)/shard_map/all_to_all | solution.py:376
  (19 shorter events, 0.1 us)
Async XLA Ops:
  0.6 10.6 %copy-start.2 = (bf16[24,4,512]{2,1,0:T(4,128)(2,1)S(1)}, bf16[24,4,512]{2,1,0:T(4,128)(2,1)}, u32[]{:S(2)}) copy-start(bf16[24,4,512]{2,1,0:T(4,128)(2,1)} %own.1) | copy-start | bytes 294916
  0.6 10.6 %copy-start.5 = (bf16[512]{0:T(512)(128)(2,1)S(1)}, bf16[512]{0:T(512)(128)(2,1)}, u32[]{:S(2)}) copy-start(bf16[512]{0:T(512)(128)(2,1)} %gain.3) | copy-start | bytes 3076
  0.7 10.6 %copy-start.1 = (bf16[7,7,512]{2,1,0:T(8,128)(2,1)S(1)}, bf16[7,7,512]{2,1,0:T(8,128)(2,1)}, u32[]{:S(2)}) copy-start(bf16[7,7,512]{2,1,0:T(8,128)(2,1)} %dw_kernel.3) | copy-start | bytes 150532
  0.7 10.6 %copy-start.7 = (bf16[512]{0:T(512)(128)(2,1)S(1)}, bf16[512]{0:T(512)(128)(2,1)}, u32[]{:S(2)}) copy-start(bf16[512]{0:T(512)(128)(2,1)} %shift.1) | copy-start | bytes 3076
  0.7 10.6 %copy-start.6 = (bf16[512]{0:T(512)(128)(2,1)S(1)}, bf16[512]{0:T(512)(128)(2,1)}, u32[]{:S(2)}) copy-start(bf16[512]{0:T(512)(128)(2,1)} %dw_bias.1) | copy-start | bytes 3076
  0.7 13.0 %copy-start = (bf16[1024,2048]{1,0:T(8,128)(2,1)S(1)}, bf16[1024,2048]{1,0:T(8,128)(2,1)}, u32[]{:S(2)}) copy-start(bf16[1024,2048]{1,0:T(8,128)(2,1)} %up.3) | copy-start | bytes 12582916
  0.7 13.0 %copy-start.4 = (bf16[2048]{0:T(1024)(128)(2,1)S(1)}, bf16[2048]{0:T(1024)(128)(2,1)}, u32[]{:S(2)}) copy-start(bf16[2048]{0:T(1024)(128)(2,1)} %up_bias.1) | copy-start | bytes 12292
  0.7 10.5 %collective-permute-start = (bf16[24,4,512]{2,1,0:T(4,128)(2,1)}, bf16[24,4,512]{2,1,0:T(4,128)(2,1)S(1)}, u32[]{:S(2)}, u32[]{:S(2)}) collective-permute-start(bf16[24,4,512]{2,1,0:T(4,128)(2,1)} %own.1), channel_id=1, source_target_pairs={{0,2},{2,4},{4,6},{6,8},{8,10},{10,12},{12,14},{1,3},{3,5},{5,7},{... | collective-permute-start | bytes 294920 | tf_op jit(solution)/shard_map/ppermute | solution.py:287
  4.4 6.8 %collective-permute-start.1 = (bf16[24,4,512]{2,1,0:T(4,128)(2,1)}, bf16[24,4,512]{2,1,0:T(4,128)(2,1)S(1)}, u32[]{:S(2)}, u32[]{:S(2)}) collective-permute-start(bf16[24,4,512]{2,1,0:T(4,128)(2,1)} %own.1), channel_id=1, source_target_pairs={{2,0},{4,2},{6,4},{8,6},{10,8},{12,10},{14,12},{3,1},{5,3},{7,5},{... | collective-permute-start | bytes 294920 | tf_op jit(solution)/shard_map/ppermute | solution.py:288
  12.1 1.5 %collective-permute-start.2 = (f32[104,512]{1,0:T(8,128)S(1)}, f32[104,512]{1,0:T(8,128)S(1)}, u32[]{:S(2)}, u32[]{:S(2)}) collective-permute-start(f32[104,512]{1,0:T(8,128)S(1)} %get-tuple-element.21.own), channel_id=1, source_target_pairs={{0,1},{1,0},{2,3},{3,2},{4,5},{5,4},{6,7},{7,6},{8,9},{9,8},{10,11... | collective-permute-start | bytes 638984 | tf_op jit(solution)/shard_map/ppermute | solution.py:346
  15.6 2.2 %copy-start.3 = (bf16[1024]{0:T(1024)(128)(2,1)S(1)}, bf16[1024]{0:T(1024)(128)(2,1)}, u32[]{:S(2)}) copy-start(bf16[1024]{0:T(1024)(128)(2,1)} %layer_scale.3) | copy-start | bytes 6148
  15.7 2.2 %copy-start.8 = (bf16[512]{0:T(512)(128)(2,1)S(1)}, bf16[512]{0:T(512)(128)(2,1)}, u32[]{:S(2)}) copy-start(bf16[512]{0:T(512)(128)(2,1)} %down_bias.1) | copy-start | bytes 3076
  15.7 2.2 %collective-permute-start.3 = (f32[96,512]{1,0:T(8,128)S(1)}, f32[96,512]{1,0:T(8,128)S(1)}, u32[]{:S(2)}, u32[]{:S(2)}) collective-permute-start(f32[96,512]{1,0:T(8,128)S(1)} %get-tuple-element.25), channel_id=1, source_target_pairs={{0,1},{1,0},{2,3},{3,2},{4,5},{5,4},{6,7},{7,6},{8,9},{9,8},{10,11... | collective-permute-start | bytes 589832 | tf_op jit(solution)/shard_map/ppermute | solution.py:361
  17.3 7.2 %collective-permute-start.4 = (bf16[96,640]{1,0:T(8,128)(2,1)S(1)}, bf16[96,640]{1,0:T(8,128)(2,1)S(1)}, u32[]{:S(2)}, u32[]{:S(2)}) collective-permute-start(bf16[96,640]{1,0:T(8,128)(2,1)S(1)} %get-tuple-element.31), channel_id=1, source_target_pairs={{0,1},{1,0},{2,3},{3,2},{4,5},{5,4},{6,7},{7,6},{8,9},{9,8},{10,11... | collective-permute-start | bytes 368648 | tf_op jit(solution)/shard_map/ppermute | solution.py:368
  18.6 16.4 %all-to-all-start = ((bf16[24,4,512]{2,1,0:T(4,128)(2,1)}), bf16[24,4,512]{2,1,0:T(4,128)(2,1)S(1)}, u32[]{:S(2)}, u32[]{:S(2)}) async-start(bf16[24,4,512]{2,1,0:T(4,128)(2,1)} %join.1), calls=%async_computation | async-start | bytes 196608 | tf_op jit(solution)/shard_map/all_to_all | solution.py:376
  24.8 4.6 %collective-permute-start.5 = (bf16[72,512]{1,0:T(8,128)(2,1)S(1)}, bf16[72,512]{1,0:T(8,128)(2,1)S(1)}, u32[]{:S(2)}, u32[]{:S(2)}) collective-permute-start(bf16[72,512]{1,0:T(8,128)(2,1)S(1)} %get-tuple-element.35), channel_id=1, source_target_pairs={{0,2},{2,0},{4,6},{6,4},{8,10},{10,8},{12,14},{14,12},{1,3},{3,1},... | collective-permute-start | bytes 221192 | tf_op jit(solution)/shard_map/ppermute | solution.py:384
  26.3 7.1 %collective-permute-start.6 = (bf16[72,512]{1,0:T(8,128)(2,1)S(1)}, bf16[72,512]{1,0:T(8,128)(2,1)S(1)}, u32[]{:S(2)}, u32[]{:S(2)}) collective-permute-start(bf16[72,512]{1,0:T(8,128)(2,1)S(1)} %get-tuple-element.36), channel_id=1, source_target_pairs={{0,0},{2,4},{4,2},{6,8},{8,6},{10,12},{12,10},{14,14},{1,1},{3,5},... | collective-permute-start | bytes 221192 | tf_op jit(solution)/shard_map/ppermute | solution.py:385

commit v3 on v2

--- a/solution.py
+++ b/solution.py
@@ -50,7 +50,7 @@
 
 
 def setup_kernel(
-    timestep, label, time_table, class_table, layer_scale, down, time_out, class_out, slope_out, down_out,
+    timestep, label, time_table, class_table, layer_scale, down, time_out, class_out, direction_out, down_out,
     step, kind, table, scale, rows8, sems, *, images, half
 ):
     pairs = ((timestep, step), (label, kind), (class_table, table), (layer_scale, scale), (down, down_out))
@@ -73,13 +73,16 @@
     for i in range(images):
         class_out[i : i + 1, :] = row_of(part, kind[i])
     fill = [jnp.zeros_like(full[0])] * (8 - images)
-    direction = (jnp.concatenate(full + fill, axis=0) * vec(scale)).astype(jnp.bfloat16)
+    direction_out[...] = (jnp.concatenate(full + fill, axis=0) * vec(scale)).astype(jnp.bfloat16)
     for i in range(images):
         copies[len(pairs) + i].wait()
         time_out[i : i + 1, :] = row_of(rows8[i].astype(jnp.float32), step[i] % 8)
     copies[4].wait()
+
+
+def slope_kernel(direction, down, slope_out):
     slope_out[...] = lax.dot_general(
-        direction, down_out[...], (((1,), (1,)), ((), ())), preferred_element_type=jnp.float32
+        direction[...], down[...], (((1,), (1,)), ((), ())), preferred_element_type=jnp.float32
     )
 
 
@@ -116,15 +119,21 @@
 
 
 def mix_kernel(
-    own, left, right, time_rows, dw_kernel, dw_bias, gain, shift, mixed_out, start_out, flat, cols, taps,
+    own, inner, outer, time_rows, dw_kernel, dw_bias, gain, shift, mixed_out, start_out, flat, cols, taps,
     *, images, high, width
 ):
     rows = images * high
     position = lax.axis_index("rows")
+    odd = position % 2 == 1
     load_taps(dw_kernel, taps)
-    for side, ref in enumerate((left, own, right)):
+    for side in range(3):
         for r in range(rows):
-            cell = ref[r].astype(jnp.float32)
+            if side == 1:
+                cell = own[r].astype(jnp.float32)
+            else:
+                near = inner[r].astype(jnp.float32)
+                far = outer[r].astype(jnp.float32)
+                cell = jnp.where(odd, near, far) if side == 0 else jnp.where(odd, far, near)
             for l in range(flat.shape[0]):
                 flat[l, r * width : (r + 1) * width, :] = cell[:, l * LANES : (l + 1) * LANES]
         for c in range(width):
@@ -282,11 +291,15 @@
         gradient_out[r] = take(flat, r * width, width, 1)
 
 
-def neighbours(first, second, axis):
+def pair_exchange(inner, outer, axis):
     count = lax.axis_size(axis)
-    from_left = lax.ppermute(first, axis, [(i, i + 1) for i in range(count - 1)])
-    from_right = lax.ppermute(second, axis, [(i + 1, i) for i in range(count - 1)])
-    return from_left, from_right
+    with jax.named_scope("inner"):
+        inner = lax.ppermute(inner, axis, [(i, i ^ 1) for i in range(count)])
+    with jax.named_scope("outer"):
+        outer = lax.ppermute(
+            outer, axis, [(i, min(max(((i + 1) ^ 1) - 1, 0), count - 1)) for i in range(count)]
+        )
+    return inner, outer
 
 
 def per_device(
@@ -316,10 +329,11 @@
     sizes = dict(images=images, high=high, width=width)
     swap = [(0, 1), (1, 0)]
 
-    left, right = neighbours(latents, latents, "rows")
-    time_rows, class_rows, slope, down = call(
+    with jax.named_scope("latent_halo"):
+        inner, outer = pair_exchange(latents, latents, "rows")
+    time_rows, class_rows, direction, down = call(
         functools.partial(setup_kernel, images=images, half=half),
-        [((8, half), f32), ((8, half), f32), ((8, hidden_size), f32), (down_weight.shape, bf16)],
+        [((8, half), f32), ((8, half), f32), ((8, full), bf16), (down_weight.shape, bf16)],
         [(a, pltpu.HBM) for a in (timestep, label, time_table, class_table, layer_scale, down_weight)],
         [
             pltpu.SMEM(timestep.shape, jnp.int32),
@@ -330,12 +344,11 @@
             pltpu.SemaphoreType.DMA((5 + images,)),
         ],
         name="setup",
-        flops=2 * 96 * full * hidden_size,
     )
     mixed, start = call(
         functools.partial(mix_kernel, **sizes),
         [((tokens + 8, half), f32), ((tokens, half), f32)],
-        [latents, left, right, time_rows, dw_kernel, dw_bias, ln_gain, ln_bias],
+        [latents, inner, outer, time_rows, dw_kernel, dw_bias, ln_gain, ln_bias],
         [
             pltpu.VMEM((half // LANES, tokens, LANES), f32),
             pltpu.VMEM((width + 6, rows, half), f32),
@@ -344,6 +357,8 @@
         name="mix",
     )
     mixed_other = lax.ppermute(mixed, "chan", swap)
+    direction, _ = lax.optimization_barrier((direction, mixed))
+    (slope,) = call(slope_kernel, [((8, hidden_size), f32)], [direction, down], name="slope")
     branch, branch_send, hidden_grad, normed, normed_other, inverse = call(
         functools.partial(forward_kernel, full=full, chunk=512, **sizes),
         [
@@ -373,16 +388,16 @@
         [pltpu.VMEM((half // LANES, tokens, LANES), f32)],
         name="join",
     )
-    features = lax.all_to_all(features, "rows", split_axis=0, concat_axis=1, tiled=True)
+    with jax.named_scope("spread"):
+        features = lax.all_to_all(features, "rows", split_axis=0, concat_axis=1, tiled=True)
     mixed_grad, inner, outer = call(
         functools.partial(norm_grad_kernel, rows=rows, full=full),
         [((tokens, half), f32), ((3 * rows, half), bf16), ((3 * rows, half), bf16)],
         [grad, grad_other, sums, normed, inverse, ln_gain],
         name="norm_grad",
     )
-    count = lax.axis_size("rows")
-    inner = lax.ppermute(inner, "rows", [(i, i ^ 1) for i in range(count)])
-    outer = lax.ppermute(outer, "rows", [(i, min(max((i + 1 ^ 1) - 1, 0), count - 1)) for i in range(count)])
+    with jax.named_scope("grad_halo"):
+        inner, outer = pair_exchange(inner, outer, "rows")
     (gradient,) = call(
         functools.partial(unmix_kernel, **sizes),
         [((rows, width, half), f32)],

time: 36 us -> 33.9 us (0.942)
  starting transfers between devices: 17.2 us -> 13.1 us
  waiting for transfers between devices: 6.67 us -> 8.69 us
    ppermute x4, starting transfers between devices: 10.5 us -> 7.1 us  [the longest x2 3.99 us: pair_exchange(): lax.ppermute(outer, axis, [(i, min(max((i + 1 ^ 1) - 1, 0), count - 1)) f...]
    ppermute x4, waiting for transfers between devices: 5.21 us -> 8.42 us  [the longest x2 7.29 us: pair_exchange(): lax.ppermute(outer, axis, [(i, min(max((i + 1 ^ 1) - 1, 0), count - 1)) f...]
    ppermute x1, waiting for transfers between devices: 1.45 us -> 0.26 us  [per_device(): mixed_other = lax.ppermute(mixed, 'chan', swap)]
    all_to_all x1, starting transfers between devices: 6.02 us -> 5.32 us  [per_device(): lax.all_to_all(features, 'rows', split_axis=0, concat_axis=1, tiled=True)]
    pallas_call x7 -> x8, Pallas kernels: 10.2 us -> 10.2 us  [call(): pl.pallas_call(body, out_shape=tuple((jax.ShapeDtypeStruct(s, d) for s, d...]
  transfers between devices with their start and end apart: 8 -> 8, of which waited for: 3 -> 4; matrix products, arithmetic and copies ran while one was open for 0% -> 0% of each run, Pallas kernels for 21% -> 22%
where the time goes in v3:
time: 33.9 us; the launch traced here: 33.6 us
  starting transfers between devices  13.1 us (39%)
  Pallas kernels  10.2 us (30%)
  waiting for transfers between devices  8.69 us (26%)
  between operations  0.8 us (2%)
  local copies, waits for them, and re-layouts  0.75 us (2%)
    pallas_call x8, Pallas kernels, call(): pl.pallas_call(body, out_shape=tuple((jax.ShapeDtypeStruct(s, d) for s, d...  10.2 us
    ppermute x2, waiting for transfers between devices, pair_exchange(): lax.ppermute(outer, axis, [(i, min(max((i + 1 ^ 1) - 1, 0), count - 1)) f...  7.29 us
    all_to_all x1, starting transfers between devices, per_device(): lax.all_to_all(features, 'rows', split_axis=0, concat_axis=1, tiled=True)  5.32 us
    ppermute x2, starting transfers between devices, pair_exchange(): lax.ppermute(outer, axis, [(i, min(max((i + 1 ^ 1) - 1, 0), count - 1)) f...  3.99 us
    ppermute x2, starting transfers between devices, pair_exchange(): inner = lax.ppermute(inner, axis, [(i, i ^ 1) for i in range(count)])  3.11 us
    ppermute x2, waiting for transfers between devices, pair_exchange(): inner = lax.ppermute(inner, axis, [(i, i ^ 1) for i in range(count)])  1.13 us
    all_to_all x2, local copies, waits for them, and re-layouts, per_device(): lax.all_to_all(features, 'rows', split_axis=0, concat_axis=1, tiled=True)  0.7 us
  transfers between devices with their start and end apart: 8, of which 4 were waited for; matrix products, arithmetic and copies ran while one was open for 0% of the time, Pallas kernels for 22%

profile of v3, /device:TPU:8, one launch (start us, length us, event | category | flops | bytes accessed | tf_op | source)
XLA Modules:
  0.0 33.6 jit_solution(6610783127523989591)
XLA Ops:
  0.7 1.6 %collective-permute-start = (bf16[24,4,512]{2,1,0:T(4,128)(2,1)}, bf16[24,4,512]{2,1,0:T(4,128)(2,1)S(1)}, u32[]{:S(2)}, u32[]{:S(2)}) collective-permute-start(bf16[24,4,512]{2,1,0:T(4,128)(2,1)} %own.1), channel_id=1, source_target_pairs={{0,2},{2,0},{4,6},{6,4},{8,10},{10,8},{12,14},{14,12},{1,3},{3,1},... | collective-permute-start | bytes 294920 | tf_op jit(solution)/shard_map/latent_halo/inner/ppermute | solution.py:297
  2.3 2.1 %collective-permute-start.1 = (bf16[24,4,512]{2,1,0:T(4,128)(2,1)}, bf16[24,4,512]{2,1,0:T(4,128)(2,1)S(1)}, u32[]{:S(2)}, u32[]{:S(2)}) collective-permute-start(bf16[24,4,512]{2,1,0:T(4,128)(2,1)} %own.1), channel_id=1, source_target_pairs={{0,0},{2,4},{4,2},{6,8},{8,6},{10,12},{12,10},{14,14},{1,1},{3,5},... | collective-permute-start | bytes 294920 | tf_op jit(solution)/shard_map/latent_halo/outer/ppermute | solution.py:299
  4.4 2.3 %setup.1 = (f32[8,512]{1,0:T(8,128)S(1)}, f32[8,512]{1,0:T(8,128)S(1)}, bf16[8,1024]{1,0:T(8,128)(2,1)S(1)}, bf16[2048,1024]{1,0:T(8,128)(2,1)S(1)}) custom-call(s32[3]{0:T(128)} %timestep.1, s32[3]{0:T(128)} %label.1, bf16[1000,512]{1,0:T(8,128)(2,1)} %time_table.1, bf16[16,1024]{1,0:T(8,128)(2,1)} %class_table.1, bf16[1024]{0:T(1024)(128)(2,1)} %layer_scale.3, ...), custom_call_target="tpu_custom_call" | custom-call | tf_op jit(solution)/shard_map/setup/pallas_call | solution.py:26
  6.7 0.0 collective-permute-done.inner
  6.7 3.2 %collective-permute-done.1.outer = bf16[24,4,512]{2,1,0:T(4,128)(2,1)S(1)} collective-permute-done((bf16[24,4,512]{2,1,0:T(4,128)(2,1)}, bf16[24,4,512]{2,1,0:T(4,128)(2,1)S(1)}, u32[]{:S(2)}, u32[]{:S(2)}) %collective-permute-start.1) | collective-permute-done | bytes 98336 | tf_op jit(solution)/shard_map/latent_halo/outer/ppermute | solution.py:299
  9.9 0.9 %mix.1 = (f32[104,512]{1,0:T(8,128)S(1)}, f32[96,512]{1,0:T(8,128)S(1)}) custom-call(bf16[24,4,512]{2,1,0:T(4,128)(2,1)S(1)} %copy-done.2, bf16[24,4,512]{2,1,0:T(4,128)(2,1)S(1)} %collective-permute-done.inner, bf16[24,4,512]{2,1,0:T(4,128)(2,1)S(1)} %collective-permute-done.1.outer, f32[8,512]{1,0:T(8,128)S(1)} %get-tuple-element.21.time_rows, ...), custom_call_target="tpu_custom_call" | custom-call | tf_op jit(solution)/shard_map/mix/pallas_call | solution.py:26
  10.8 0.1 collective-permute-start.2
  10.9 1.2 %slope.1 = f32[8,2048]{1,0:T(8,128)S(1)} custom-call(bf16[8,1024]{1,0:T(8,128)(2,1)S(1)} %get-tuple-element.24.direction, bf16[2048,1024]{1,0:T(8,128)(2,1)S(1)} %get-tuple-element.25.down), custom_call_target="tpu_custom_call" | custom-call | tf_op jit(solution)/shard_map/slope/pallas_call | solution.py:26
  12.1 0.3 collective-permute-done.2.other
  12.3 2.0 %forward.1 = (f32[96,512]{1,0:T(8,128)S(1)}, f32[96,512]{1,0:T(8,128)S(1)}, bf16[96,2048]{1,0:T(8,128)(2,1)S(1)}, f32[96,512]{1,0:T(8,128)S(1)}, f32[96,512]{1,0:T(8,128)S(1)}, /*index=5*/f32[96,128]{1,0:T(8,128)S(1)}) custom-call(f32[104,512]{1,0:T(8,128)S(1)} %get-tuple-element.22.own, f32[104,512]{1,0:T(8,128)S(1)} %collective-permute-done.2.other, ...), custom_call_target="tpu_custom_call" | custom-call | tf_op jit(solution)/shard_map/forward/pallas_call | solution.py:26
  14.3 0.0 copy-start.3
  14.3 0.0 copy-start.8
  14.3 0.3 collective-permute-start.3
  14.6 1.5 %backward.1 = (f32[96,512]{1,0:T(8,128)S(1)}, bf16[96,640]{1,0:T(8,128)(2,1)S(1)}, f32[96,128]{1,0:T(8,128)S(1)}) custom-call(bf16[96,2048]{1,0:T(8,128)(2,1)S(1)} %get-tuple-element.29.hidden_grad, bf16[1024,2048]{1,0:T(8,128)(2,1)S(1)} %copy-done, f32[104,512]{1,0:T(8,128)S(1)} %get-tuple-element.22.own, f32[104,512]{1,0:T(8,128)S(1)} %collective-permute-done.2.other, ...), custom_call_target="tpu_custom_call" | custom-call | tf_op jit(solution)/shard_map/backward/pallas_call | solution.py:26
  16.1 0.3 %collective-permute-start.4 = (bf16[96,640]{1,0:T(8,128)(2,1)S(1)}, bf16[96,640]{1,0:T(8,128)(2,1)S(1)}, u32[]{:S(2)}, u32[]{:S(2)}) collective-permute-start(bf16[96,640]{1,0:T(8,128)(2,1)S(1)} %get-tuple-element.33), channel_id=1, source_target_pairs={{0,1},{1,0},{2,3},{3,2},{4,5},{5,4},{6,7},{7,6},{8,9},{9,8},{10,11... | collective-permute-start | bytes 368648 | tf_op jit(solution)/shard_map/ppermute | solution.py:383
  16.5 0.7 %join.1 = bf16[24,4,512]{2,1,0:T(4,128)(2,1)} custom-call(f32[96,512]{1,0:T(8,128)S(1)} %get-tuple-element.26.branch, f32[96,512]{1,0:T(8,128)S(1)} %collective-permute-done.3.branch_other, f32[96,512]{1,0:T(8,128)S(1)} %get-tuple-element.28.start, bf16[512]{0:T(512)(128)(2,1)S(1)} %copy-done.8, bf16[1024]{0:T(1024)(128)(2,1)S(1)} %copy-done.3), custom_call_target="tpu_custom_call" | custom-call | tf_op jit(solution)/shard_map/join/pallas_call | solution.py:26
  17.2 5.3 %all-to-all-start = ((bf16[24,4,512]{2,1,0:T(4,128)(2,1)}), bf16[24,4,512]{2,1,0:T(4,128)(2,1)S(1)}, u32[]{:S(2)}, u32[]{:S(2)}) async-start(bf16[24,4,512]{2,1,0:T(4,128)(2,1)} %join.1), calls=%async_computation | async-start | bytes 196608 | tf_op jit(solution)/shard_map/spread/all_to_all | solution.py:392
  22.5 0.2 norm_grad.1
  22.7 1.5 %collective-permute-start.5 = (bf16[72,512]{1,0:T(8,128)(2,1)S(1)}, bf16[72,512]{1,0:T(8,128)(2,1)S(1)}, u32[]{:S(2)}, u32[]{:S(2)}) collective-permute-start(bf16[72,512]{1,0:T(8,128)(2,1)S(1)} %get-tuple-element.37), channel_id=1, source_target_pairs={{0,2},{2,0},{4,6},{6,4},{8,10},{10,8},{12,14},{14,12},{1,3},{3,1},... | collective-permute-start | bytes 221192 | tf_op jit(solution)/shard_map/grad_halo/inner/ppermute | solution.py:297
  24.3 1.9 %collective-permute-start.6 = (bf16[72,512]{1,0:T(8,128)(2,1)S(1)}, bf16[72,512]{1,0:T(8,128)(2,1)S(1)}, u32[]{:S(2)}, u32[]{:S(2)}) collective-permute-start(bf16[72,512]{1,0:T(8,128)(2,1)S(1)} %get-tuple-element.38), channel_id=1, source_target_pairs={{0,0},{2,4},{4,2},{6,8},{8,6},{10,12},{12,10},{14,14},{1,1},{3,5},... | collective-permute-start | bytes 221192 | tf_op jit(solution)/shard_map/grad_halo/outer/ppermute | solution.py:299
  26.2 1.1 %collective-permute-done.5.inner = bf16[72,512]{1,0:T(8,128)(2,1)S(1)} collective-permute-done((bf16[72,512]{1,0:T(8,128)(2,1)S(1)}, bf16[72,512]{1,0:T(8,128)(2,1)S(1)}, u32[]{:S(2)}, u32[]{:S(2)}) %collective-permute-start.5) | collective-permute-done | bytes 73760 | tf_op jit(solution)/shard_map/grad_halo/inner/ppermute | solution.py:297
  27.3 4.1 %collective-permute-done.6.outer = bf16[72,512]{1,0:T(8,128)(2,1)S(1)} collective-permute-done((bf16[72,512]{1,0:T(8,128)(2,1)S(1)}, bf16[72,512]{1,0:T(8,128)(2,1)S(1)}, u32[]{:S(2)}, u32[]{:S(2)}) %collective-permute-start.6) | collective-permute-done | bytes 73760 | tf_op jit(solution)/shard_map/grad_halo/outer/ppermute | solution.py:299
  31.4 1.5 %unmix.1 = f32[24,4,512]{2,1,0:T(4,128)} custom-call(f32[96,512]{1,0:T(8,128)S(1)} %get-tuple-element.36.own, bf16[72,512]{1,0:T(8,128)(2,1)S(1)} %collective-permute-done.5.inner, bf16[72,512]{1,0:T(8,128)(2,1)S(1)} %collective-permute-done.6.outer, f32[8,512]{1,0:T(8,128)S(1)} %get-tuple-element.39.class_rows, bf16[7,7,512]{2,1,0:T(8,128)(2,1)S(1)} %copy-done.1), custom_call_target="tpu_custom_call" | custom-call | tf_op jit(solution)/shard_map/unmix/pallas_call | solution.py:26
  32.9 0.7 %all_to_all.16 = bf16[3,32,512]{2,1,0:T(8,128)(2,1)} reshape(bf16[3,8,4,512]{3,2,1,0:T(4,128)(2,1)S(1)} %copy.16) | data formatting | bytes 196608 | tf_op jit(solution)/shard_map/spread/all_to_all | solution.py:392
  (20 shorter events, 0.1 us)
Async XLA Ops:
  0.6 9.3 %copy-start.2 = (bf16[24,4,512]{2,1,0:T(4,128)(2,1)S(1)}, bf16[24,4,512]{2,1,0:T(4,128)(2,1)}, u32[]{:S(2)}) copy-start(bf16[24,4,512]{2,1,0:T(4,128)(2,1)} %own.1) | copy-start | bytes 294916
  0.6 9.3 %copy-start.5 = (bf16[512]{0:T(512)(128)(2,1)S(1)}, bf16[512]{0:T(512)(128)(2,1)}, u32[]{:S(2)}) copy-start(bf16[512]{0:T(512)(128)(2,1)} %gain.3) | copy-start | bytes 3076
  0.7 9.3 %copy-start.1 = (bf16[7,7,512]{2,1,0:T(8,128)(2,1)S(1)}, bf16[7,7,512]{2,1,0:T(8,128)(2,1)}, u32[]{:S(2)}) copy-start(bf16[7,7,512]{2,1,0:T(8,128)(2,1)} %dw_kernel.3) | copy-start | bytes 150532
  0.7 9.2 %copy-start.7 = (bf16[512]{0:T(512)(128)(2,1)S(1)}, bf16[512]{0:T(512)(128)(2,1)}, u32[]{:S(2)}) copy-start(bf16[512]{0:T(512)(128)(2,1)} %shift.1) | copy-start | bytes 3076
  0.7 9.2 %copy-start.6 = (bf16[512]{0:T(512)(128)(2,1)S(1)}, bf16[512]{0:T(512)(128)(2,1)}, u32[]{:S(2)}) copy-start(bf16[512]{0:T(512)(128)(2,1)} %dw_bias.1) | copy-start | bytes 3076
  0.7 11.6 %copy-start = (bf16[1024,2048]{1,0:T(8,128)(2,1)S(1)}, bf16[1024,2048]{1,0:T(8,128)(2,1)}, u32[]{:S(2)}) copy-start(bf16[1024,2048]{1,0:T(8,128)(2,1)} %up.3) | copy-start | bytes 12582916
  0.7 11.6 %copy-start.4 = (bf16[2048]{0:T(1024)(128)(2,1)S(1)}, bf16[2048]{0:T(1024)(128)(2,1)}, u32[]{:S(2)}) copy-start(bf16[2048]{0:T(1024)(128)(2,1)} %up_bias.1) | copy-start | bytes 12292
  0.7 6.0 %collective-permute-start = (bf16[24,4,512]{2,1,0:T(4,128)(2,1)}, bf16[24,4,512]{2,1,0:T(4,128)(2,1)S(1)}, u32[]{:S(2)}, u32[]{:S(2)}) collective-permute-start(bf16[24,4,512]{2,1,0:T(4,128)(2,1)} %own.1), channel_id=1, source_target_pairs={{0,2},{2,0},{4,6},{6,4},{8,10},{10,8},{12,14},{14,12},{1,3},{3,1},... | collective-permute-start | bytes 294920 | tf_op jit(solution)/shard_map/latent_halo/inner/ppermute | solution.py:297
  2.3 7.6 %collective-permute-start.1 = (bf16[24,4,512]{2,1,0:T(4,128)(2,1)}, bf16[24,4,512]{2,1,0:T(4,128)(2,1)S(1)}, u32[]{:S(2)}, u32[]{:S(2)}) collective-permute-start(bf16[24,4,512]{2,1,0:T(4,128)(2,1)} %own.1), channel_id=1, source_target_pairs={{0,0},{2,4},{4,2},{6,8},{8,6},{10,12},{12,10},{14,14},{1,1},{3,5},... | collective-permute-start | bytes 294920 | tf_op jit(solution)/shard_map/latent_halo/outer/ppermute | solution.py:299
  10.8 1.5 %collective-permute-start.2 = (f32[104,512]{1,0:T(8,128)S(1)}, f32[104,512]{1,0:T(8,128)S(1)}, u32[]{:S(2)}, u32[]{:S(2)}) collective-permute-start(f32[104,512]{1,0:T(8,128)S(1)} %get-tuple-element.22.own), channel_id=1, source_target_pairs={{0,1},{1,0},{2,3},{3,2},{4,5},{5,4},{6,7},{7,6},{8,9},{9,8},{10,11... | collective-permute-start | bytes 638984 | tf_op jit(solution)/shard_map/ppermute | solution.py:359
  14.3 2.2 %copy-start.3 = (bf16[1024]{0:T(1024)(128)(2,1)S(1)}, bf16[1024]{0:T(1024)(128)(2,1)}, u32[]{:S(2)}) copy-start(bf16[1024]{0:T(1024)(128)(2,1)} %layer_scale.3) | copy-start | bytes 6148
  14.3 2.2 %copy-start.8 = (bf16[512]{0:T(512)(128)(2,1)S(1)}, bf16[512]{0:T(512)(128)(2,1)}, u32[]{:S(2)}) copy-start(bf16[512]{0:T(512)(128)(2,1)} %down_bias.1) | copy-start | bytes 3076
  14.3 2.2 %collective-permute-start.3 = (f32[96,512]{1,0:T(8,128)S(1)}, f32[96,512]{1,0:T(8,128)S(1)}, u32[]{:S(2)}, u32[]{:S(2)}) collective-permute-start(f32[96,512]{1,0:T(8,128)S(1)} %get-tuple-element.27), channel_id=1, source_target_pairs={{0,1},{1,0},{2,3},{3,2},{4,5},{5,4},{6,7},{7,6},{8,9},{9,8},{10,11... | collective-permute-start | bytes 589832 | tf_op jit(solution)/shard_map/ppermute | solution.py:376
  16.1 6.4 %collective-permute-start.4 = (bf16[96,640]{1,0:T(8,128)(2,1)S(1)}, bf16[96,640]{1,0:T(8,128)(2,1)S(1)}, u32[]{:S(2)}, u32[]{:S(2)}) collective-permute-start(bf16[96,640]{1,0:T(8,128)(2,1)S(1)} %get-tuple-element.33), channel_id=1, source_target_pairs={{0,1},{1,0},{2,3},{3,2},{4,5},{5,4},{6,7},{7,6},{8,9},{9,8},{10,11... | collective-permute-start | bytes 368648 | tf_op jit(solution)/shard_map/ppermute | solution.py:383
  17.2 15.7 %all-to-all-start = ((bf16[24,4,512]{2,1,0:T(4,128)(2,1)}), bf16[24,4,512]{2,1,0:T(4,128)(2,1)S(1)}, u32[]{:S(2)}, u32[]{:S(2)}) async-start(bf16[24,4,512]{2,1,0:T(4,128)(2,1)} %join.1), calls=%async_computation | async-start | bytes 196608 | tf_op jit(solution)/shard_map/spread/all_to_all | solution.py:392
  22.7 4.6 %collective-permute-start.5 = (bf16[72,512]{1,0:T(8,128)(2,1)S(1)}, bf16[72,512]{1,0:T(8,128)(2,1)S(1)}, u32[]{:S(2)}, u32[]{:S(2)}) collective-permute-start(bf16[72,512]{1,0:T(8,128)(2,1)S(1)} %get-tuple-element.37), channel_id=1, source_target_pairs={{0,2},{2,0},{4,6},{6,4},{8,10},{10,8},{12,14},{14,12},{1,3},{3,1},... | collective-permute-start | bytes 221192 | tf_op jit(solution)/shard_map/grad_halo/inner/ppermute | solution.py:297
  24.3 7.1 %collective-permute-start.6 = (bf16[72,512]{1,0:T(8,128)(2,1)S(1)}, bf16[72,512]{1,0:T(8,128)(2,1)S(1)}, u32[]{:S(2)}, u32[]{:S(2)}) collective-permute-start(bf16[72,512]{1,0:T(8,128)(2,1)S(1)} %get-tuple-element.38), channel_id=1, source_target_pairs={{0,0},{2,4},{4,2},{6,8},{8,6},{10,12},{12,10},{14,14},{1,1},{3,5},... | collective-permute-start | bytes 221192 | tf_op jit(solution)/shard_map/grad_halo/outer/ppermute | solution.py:299

commit v4 on v3

--- a/solution.py
+++ b/solution.py
@@ -86,78 +86,100 @@
     )
 
 
-def stencil(cols, taps, store, flip, images, high, width):
+def stencil(cols, places, taps, base, store, flip, images, high, width):
     channels = cols.shape[2]
     row = lax.broadcasted_iota(jnp.int32, (high, LANES), 0)
     inside = [(row + (t - 3) >= 0) & (row + (t - 3) < high) for t in range(7)]
     for lane in range(0, channels, LANES):
         for image in range(images):
             first = image * high
-            column = [cols[c, first : first + high, lane : lane + LANES] for c in range(width + 6)]
-            total = [None] * width
+            column = {p: cols[i, first : first + high, lane : lane + LANES] for i, p in enumerate(places)}
+            total = [base(c, first, lane) for c in range(width)]
             for t in range(7):
                 part = [None] * width
                 for d in range(7):
                     place = 8 * (6 - t) + 6 - d if flip else 8 * t + d
                     weight = jnp.broadcast_to(taps[place : place + 1, lane : lane + LANES], (high, LANES))
                     for c in range(width):
-                        term = column[c + d] * weight
-                        part[c] = term if d == 0 else part[c] + term
+                        if c + d in column:
+                            term = column[c + d] * weight
+                            part[c] = term if part[c] is None else part[c] + term
                 for c in range(width):
                     moved = part[c]
+                    if moved is None:
+                        continue
                     if t != 3:
                         moved = pltpu.roll(moved, (3 - t) % high, 0)
                         moved = jnp.where(inside[t], moved, 0.0)
-                    total[c] = moved if t == 0 else total[c] + moved
+                    total[c] = total[c] + moved
             for c in range(width):
                 store(c, first, lane, total[c])
 
 
-def load_taps(dw_kernel, taps):
+def own_places(width):
+    return tuple(range(3, 3 + width))
+
+
+def side_places(width):
+    return (0, 1, 2, 3 + width, 4 + width, 5 + width)
+
+
+def writer(out, rows):
+    def store(c, first, lane, value):
+        out[c * rows + first : c * rows + first + value.shape[0], lane : lane + LANES] = value
+
+    return store
+
+
+def reader(ref, rows, high):
+    return lambda c, first, lane: ref[c * rows + first : c * rows + first + high, lane : lane + LANES]
+
+
+def unpack(tile, flat, rows, width):
+    for r in range(rows):
+        cell = tile(r)
+        for l in range(flat.shape[0]):
+            flat[l, r * width : (r + 1) * width, :] = cell[:, l * LANES : (l + 1) * LANES]
+
+
+def mix_own_kernel(own, time_rows, dw_kernel, dw_bias, part_out, start_out, taps, flat, cols, *, images, high, width):
+    rows = images * high
     for t in range(7):
         taps[8 * t : 8 * t + 7, :] = dw_kernel[t].astype(jnp.float32)
-
-
-def mix_kernel(
-    own, inner, outer, time_rows, dw_kernel, dw_bias, gain, shift, mixed_out, start_out, flat, cols, taps,
-    *, images, high, width
+    unpack(lambda r: own[r].astype(jnp.float32), flat, rows, width)
+    for c in range(width):
+        for image in range(images):
+            first = image * high
+            value = take(flat, first * width + c, high, width) + time_rows[image : image + 1, :]
+            cols[c, first : first + high, :] = value
+            start_out[c * rows + first : c * rows + first + high, :] = value
+    bias = vec(dw_bias)
+    base = lambda c, first, lane: jnp.broadcast_to(bias[:, lane : lane + LANES], (high, LANES))
+    stencil(cols, own_places(width), taps, base, writer(part_out, rows), False, images, high, width)
+
+
+def mix_sides_kernel(
+    inner, outer, time_rows, taps, part, gain, shift, mixed_out, flat, cols, *, images, high, width
 ):
     rows = images * high
     position = lax.axis_index("rows")
     odd = position % 2 == 1
-    load_taps(dw_kernel, taps)
-    for side in range(3):
-        for r in range(rows):
-            if side == 1:
-                cell = own[r].astype(jnp.float32)
-            else:
-                near = inner[r].astype(jnp.float32)
-                far = outer[r].astype(jnp.float32)
-                cell = jnp.where(odd, near, far) if side == 0 else jnp.where(odd, far, near)
-            for l in range(flat.shape[0]):
-                flat[l, r * width : (r + 1) * width, :] = cell[:, l * LANES : (l + 1) * LANES]
-        for c in range(width):
-            place = (side - 1) * width + c + 3
-            if place < 0 or place >= width + 6:
-                continue
+    for side in range(2):
+        first_tile, second_tile = (inner, outer) if side == 0 else (outer, inner)
+        unpack(
+            lambda r: jnp.where(odd, first_tile[r].astype(jnp.float32), second_tile[r].astype(jnp.float32)),
+            flat, rows, width,
+        )
+        edge = position > 0 if side == 0 else position < lax.axis_size("rows") - 1
+        for i in range(3):
+            c = width - 3 + i if side == 0 else i
             for image in range(images):
                 first = image * high
                 value = take(flat, first * width + c, high, width) + time_rows[image : image + 1, :]
-                if side == 0:
-                    value = value * jnp.where(position > 0, 1.0, 0.0)
-                if side == 2:
-                    value = value * jnp.where(position < lax.axis_size("rows") - 1, 1.0, 0.0)
-                cols[place, first : first + high, :] = value
-                if side == 1:
-                    start_out[c * rows + first : c * rows + first + high, :] = value
-    bias = vec(dw_bias)
-
-    def store(c, first, lane, value):
-        mixed_out[c * rows + first : c * rows + first + high, lane : lane + LANES] = (
-            value + bias[:, lane : lane + LANES]
-        )
-
-    stencil(cols, taps, store, False, images, high, width)
+                cols[side * 3 + i, first : first + high, :] = value * jnp.where(edge, 1.0, 0.0)
+    stencil(
+        cols, side_places(width), taps, reader(part, rows, high), writer(mixed_out, rows), False, images, high, width
+    )
     tokens = rows * width
     mixed_out[tokens : tokens + 1, :] = vec(gain)
     mixed_out[tokens + 1 : tokens + 2, :] = vec(shift)
@@ -265,30 +287,41 @@
     outer_out[...] = grad_out[pl.ds(low, edge), :].astype(jnp.bfloat16)
 
 
-def unmix_kernel(own, inner, outer, class_rows, dw_kernel, gradient_out, flat, cols, taps, *, images, high, width):
+def unmix_own_kernel(own, class_rows, taps, part_out, cols, *, images, high, width):
     rows = images * high
-    load_taps(dw_kernel, taps)
+    for c in range(width):
+        cols[c] = own[c * rows : (c + 1) * rows, :]
+    classes = class_rows[...]
+
+    def base(c, first, lane):
+        image = first // high
+        return jnp.broadcast_to(classes[image : image + 1, lane : lane + LANES], (high, LANES))
+
+    stencil(cols, own_places(width), taps, base, writer(part_out, rows), True, images, high, width)
+
+
+def unmix_sides_kernel(
+    part, inner, outer, taps, features, gradient_out, features_out, flat, cols, lines, *, images, high, width
+):
+    rows = images * high
     position = lax.axis_index("rows")
     parity = position % 2
     within = (position > 0) & (position < lax.axis_size("rows") - 1)
-    inner_side = pl.multiple_of((1 - parity) * (3 + width), 1)
-    outer_side = pl.multiple_of(parity * (3 + width), 1)
     for c in range(3):
-        cols[inner_side + c] = inner[c * rows : (c + 1) * rows, :].astype(jnp.float32)
-        cols[outer_side + c] = outer[c * rows : (c + 1) * rows, :].astype(jnp.float32) * jnp.where(within, 1.0, 0.0)
-    for c in range(width):
-        cols[c + 3] = own[c * rows : (c + 1) * rows, :]
-    classes = class_rows[...]
+        cols[(1 - parity) * 3 + c] = inner[c * rows : (c + 1) * rows, :].astype(jnp.float32)
+        cols[parity * 3 + c] = outer[c * rows : (c + 1) * rows, :].astype(jnp.float32) * jnp.where(within, 1.0, 0.0)
 
     def store(c, first, lane, value):
-        image = first // high
-        flat[lane // LANES, pl.ds(first * width + c, high, stride=width), :] = (
-            value + classes[image : image + 1, lane : lane + LANES]
-        )
-
-    stencil(cols, taps, store, True, images, high, width)
+        flat[lane // LANES, pl.ds(first * width + c, high, stride=width), :] = value
+
+    stencil(cols, side_places(width), taps, reader(part, rows, high), store, True, images, high, width)
     for r in range(rows):
         gradient_out[r] = take(flat, r * width, width, 1)
+    high_out, wide_out, _ = features_out.shape
+    for j in range(high_out):
+        for block in range(wide_out // width):
+            lines[block * width : (block + 1) * width, :] = features[block * high_out + j].astype(jnp.float32)
+        features_out[j] = lines[...].astype(jnp.bfloat16)
 
 
 def pair_exchange(inner, outer, axis):
@@ -345,16 +378,20 @@
         ],
         name="setup",
     )
-    mixed, start = call(
-        functools.partial(mix_kernel, **sizes),
-        [((tokens + 8, half), f32), ((tokens, half), f32)],
-        [latents, inner, outer, time_rows, dw_kernel, dw_bias, ln_gain, ln_bias],
-        [
-            pltpu.VMEM((half // LANES, tokens, LANES), f32),
-            pltpu.VMEM((width + 6, rows, half), f32),
-            pltpu.VMEM((56, half), f32),
-        ],
-        name="mix",
+    flat = pltpu.VMEM((half // LANES, tokens, LANES), f32)
+    part, start, taps = call(
+        functools.partial(mix_own_kernel, **sizes),
+        [((tokens, half), f32), ((tokens, half), f32), ((56, half), f32)],
+        [latents, time_rows, dw_kernel, dw_bias],
+        [flat, pltpu.VMEM((width, rows, half), f32)],
+        name="mix_own",
+    )
+    (mixed,) = call(
+        functools.partial(mix_sides_kernel, **sizes),
+        [((tokens + 8, half), f32)],
+        [inner, outer, time_rows, taps, part, ln_gain, ln_bias],
+        [flat, pltpu.VMEM((6, rows, half), f32)],
+        name="mix_sides",
     )
     mixed_other = lax.ppermute(mixed, "chan", swap)
     direction, _ = lax.optimization_barrier((direction, mixed))
@@ -389,7 +426,7 @@
         name="join",
     )
     with jax.named_scope("spread"):
-        features = lax.all_to_all(features, "rows", split_axis=0, concat_axis=1, tiled=True)
+        features = lax.all_to_all(features, "rows", split_axis=0, concat_axis=0, tiled=True)
     mixed_grad, inner, outer = call(
         functools.partial(norm_grad_kernel, rows=rows, full=full),
         [((tokens, half), f32), ((3 * rows, half), bf16), ((3 * rows, half), bf16)],
@@ -398,16 +435,20 @@
     )
     with jax.named_scope("grad_halo"):
         inner, outer = pair_exchange(inner, outer, "rows")
-    (gradient,) = call(
-        functools.partial(unmix_kernel, **sizes),
-        [((rows, width, half), f32)],
-        [mixed_grad, inner, outer, class_rows, dw_kernel],
-        [
-            pltpu.VMEM((half // LANES, tokens, LANES), f32),
-            pltpu.VMEM((width + 6, rows, half), f32),
-            pltpu.VMEM((56, half), f32),
-        ],
-        name="unmix",
+    (part,) = call(
+        functools.partial(unmix_own_kernel, **sizes),
+        [((tokens, half), f32)],
+        [mixed_grad, class_rows, taps],
+        [pltpu.VMEM((width, rows, half), f32)],
+        name="unmix_own",
+    )
+    count = lax.axis_size("rows")
+    gradient, features = call(
+        functools.partial(unmix_sides_kernel, **sizes),
+        [((rows, width, half), f32), ((rows // count, width * count, half), bf16)],
+        [part, inner, outer, taps, features],
+        [flat, pltpu.VMEM((6, rows, half), f32), pltpu.VMEM((width * count, half), f32)],
+        name="unmix_sides",
     )
     return features, gradient
 

time: 33.9 us -> 32.4 us (0.956)
  waiting for transfers between devices: 8.69 us -> 7.72 us
  local copies, waits for them, and re-layouts: 0.75 us -> 0.04 us
    all_to_all x2 -> x0, local copies, waits for them, and re-layouts: 0.7 us -> none  [per_device(): lax.all_to_all(features, 'rows', split_axis=0, concat_axis=1, tiled=True)]
    ppermute x2, waiting for transfers between devices: 7.29 us -> 6.77 us  [pair_exchange(): lax.ppermute(outer, axis, [(i, min(max((i + 1 ^ 1) - 1, 0), count - 1)) f...]
    ppermute x2, waiting for transfers between devices: 1.13 us -> 0.68 us  [pair_exchange(): inner = lax.ppermute(inner, axis, [(i, i ^ 1) for i in range(count)])]
    pallas_call x8 -> x10, Pallas kernels: 10.2 us -> 10.4 us  [call(): pl.pallas_call(body, out_shape=tuple((jax.ShapeDtypeStruct(s, d) for s, d...]
  transfers between devices with their start and end apart: 8 -> 8, of which waited for: 4 -> 4; matrix products, arithmetic and copies ran while one was open for 0% -> 0% of each run, Pallas kernels for 22% -> 21%
where the time goes in v4:
time: 32.4 us; the launch traced here: 32.1 us
  starting transfers between devices  13.1 us (40%)
  Pallas kernels  10.4 us (32%)
  waiting for transfers between devices  7.72 us (24%)
  between operations  0.82 us (3%)
    pallas_call x10, Pallas kernels, call(): pl.pallas_call(body, out_shape=tuple((jax.ShapeDtypeStruct(s, d) for s, d...  10.4 us
    ppermute x2, waiting for transfers between devices, pair_exchange(): lax.ppermute(outer, axis, [(i, min(max((i + 1 ^ 1) - 1, 0), count - 1)) f...  6.77 us
    all_to_all x1, starting transfers between devices, per_device(): lax.all_to_all(features, 'rows', split_axis=0, concat_axis=0, tiled=True)  5.33 us
    ppermute x2, starting transfers between devices, pair_exchange(): lax.ppermute(outer, axis, [(i, min(max((i + 1 ^ 1) - 1, 0), count - 1)) f...  3.99 us
    ppermute x2, starting transfers between devices, pair_exchange(): inner = lax.ppermute(inner, axis, [(i, i ^ 1) for i in range(count)])  3.11 us
    ppermute x2, waiting for transfers between devices, pair_exchange(): inner = lax.ppermute(inner, axis, [(i, i ^ 1) for i in range(count)])  0.68 us
  transfers between devices with their start and end apart: 8, of which 4 were waited for; matrix products, arithmetic and copies ran while one was open for 0% of the time, Pallas kernels for 21%

profile of v4, /device:TPU:8, one launch (start us, length us, event | category | flops | bytes accessed | tf_op | source)
XLA Modules:
  0.0 32.1 jit_solution(1183873398635012856)
XLA Ops:
  0.7 1.6 %collective-permute-start = (bf16[24,4,512]{2,1,0:T(4,128)(2,1)}, bf16[24,4,512]{2,1,0:T(4,128)(2,1)S(1)}, u32[]{:S(2)}, u32[]{:S(2)}) collective-permute-start(bf16[24,4,512]{2,1,0:T(4,128)(2,1)} %own.1), channel_id=1, source_target_pairs={{0,2},{2,0},{4,6},{6,4},{8,10},{10,8},{12,14},{14,12},{1,3},{3,1},... | collective-permute-start | bytes 294920 | tf_op jit(solution)/shard_map/latent_halo/inner/ppermute | solution.py:330
  2.3 2.1 %collective-permute-start.1 = (bf16[24,4,512]{2,1,0:T(4,128)(2,1)}, bf16[24,4,512]{2,1,0:T(4,128)(2,1)S(1)}, u32[]{:S(2)}, u32[]{:S(2)}) collective-permute-start(bf16[24,4,512]{2,1,0:T(4,128)(2,1)} %own.1), channel_id=1, source_target_pairs={{0,0},{2,4},{4,2},{6,8},{8,6},{10,12},{12,10},{14,14},{1,1},{3,5},... | collective-permute-start | bytes 294920 | tf_op jit(solution)/shard_map/latent_halo/outer/ppermute | solution.py:332
  4.4 2.3 %setup.1 = (f32[8,512]{1,0:T(8,128)S(1)}, f32[8,512]{1,0:T(8,128)S(1)}, bf16[8,1024]{1,0:T(8,128)(2,1)S(1)}, bf16[2048,1024]{1,0:T(8,128)(2,1)S(1)}) custom-call(s32[3]{0:T(128)} %timestep.1, s32[3]{0:T(128)} %label.1, bf16[1000,512]{1,0:T(8,128)(2,1)} %time_table.1, bf16[16,1024]{1,0:T(8,128)(2,1)} %class_table.1, bf16[1024]{0:T(1024)(128)(2,1)} %layer_scale.3, ...), custom_call_target="tpu_custom_call" | custom-call | tf_op jit(solution)/shard_map/setup/pallas_call | solution.py:26
  6.7 0.5 %mix_own.1 = (f32[96,512]{1,0:T(8,128)S(1)}, f32[96,512]{1,0:T(8,128)S(1)}, f32[56,512]{1,0:T(8,128)S(1)}) custom-call(bf16[24,4,512]{2,1,0:T(4,128)(2,1)S(1)} %copy-done.1, f32[8,512]{1,0:T(8,128)S(1)} %get-tuple-element.24.time_rows, bf16[7,7,512]{2,1,0:T(8,128)(2,1)S(1)} %copy-done.2, bf16[512]{0:T(512)(128)(2,1)S(1)} %copy-done.6), custom_call_target="tpu_custom_call" | custom-call | tf_op jit(solution)/shard_map/mix_own/pallas_call | solution.py:26
  7.2 2.7 %collective-permute-done.1.outer = bf16[24,4,512]{2,1,0:T(4,128)(2,1)S(1)} collective-permute-done((bf16[24,4,512]{2,1,0:T(4,128)(2,1)}, bf16[24,4,512]{2,1,0:T(4,128)(2,1)S(1)}, u32[]{:S(2)}, u32[]{:S(2)}) %collective-permute-start.1) | collective-permute-done | bytes 98336 | tf_op jit(solution)/shard_map/latent_halo/outer/ppermute | solution.py:332
  9.9 0.4 %mix_sides.1.own = f32[104,512]{1,0:T(8,128)S(1)} custom-call(bf16[24,4,512]{2,1,0:T(4,128)(2,1)S(1)} %collective-permute-done.inner, bf16[24,4,512]{2,1,0:T(4,128)(2,1)S(1)} %collective-permute-done.1.outer, f32[8,512]{1,0:T(8,128)S(1)} %get-tuple-element.24.time_rows, f32[56,512]{1,0:T(8,128)S(1)} %get-tuple-element.25.taps, ...), custom_call_target="tpu_custom_call" | custom-call | tf_op jit(solution)/shard_map/mix_sides/pallas_call | solution.py:26
  10.4 0.1 collective-permute-start.2
  10.4 1.2 %slope.1 = f32[8,2048]{1,0:T(8,128)S(1)} custom-call(bf16[8,1024]{1,0:T(8,128)(2,1)S(1)} %get-tuple-element.28.direction, bf16[2048,1024]{1,0:T(8,128)(2,1)S(1)} %get-tuple-element.29.down), custom_call_target="tpu_custom_call" | custom-call | tf_op jit(solution)/shard_map/slope/pallas_call | solution.py:26
  11.6 0.3 collective-permute-done.2.other
  11.9 2.0 %forward.1 = (f32[96,512]{1,0:T(8,128)S(1)}, f32[96,512]{1,0:T(8,128)S(1)}, bf16[96,2048]{1,0:T(8,128)(2,1)S(1)}, f32[96,512]{1,0:T(8,128)S(1)}, f32[96,512]{1,0:T(8,128)S(1)}, /*index=5*/f32[96,128]{1,0:T(8,128)S(1)}) custom-call(f32[104,512]{1,0:T(8,128)S(1)} %mix_sides.1.own, f32[104,512]{1,0:T(8,128)S(1)} %collective-permute-done.2.other, ...), custom_call_target="tpu_custom_call" | custom-call | tf_op jit(solution)/shard_map/forward/pallas_call | solution.py:26
  13.8 0.0 copy-start.3
  13.9 0.0 copy-start.8
  13.9 0.3 collective-permute-start.6
  14.2 1.5 %backward.1 = (f32[96,512]{1,0:T(8,128)S(1)}, bf16[96,640]{1,0:T(8,128)(2,1)S(1)}, f32[96,128]{1,0:T(8,128)S(1)}) custom-call(bf16[96,2048]{1,0:T(8,128)(2,1)S(1)} %get-tuple-element.30.hidden_grad, bf16[1024,2048]{1,0:T(8,128)(2,1)S(1)} %copy-done, f32[104,512]{1,0:T(8,128)S(1)} %mix_sides.1.own, f32[104,512]{1,0:T(8,128)S(1)} %collective-permute-done.2.other, ...), custom_call_target="tpu_custom_call" | custom-call | tf_op jit(solution)/shard_map/backward/pallas_call | solution.py:26
  15.7 0.3 %collective-permute-start.3 = (bf16[96,640]{1,0:T(8,128)(2,1)S(1)}, bf16[96,640]{1,0:T(8,128)(2,1)S(1)}, u32[]{:S(2)}, u32[]{:S(2)}) collective-permute-start(bf16[96,640]{1,0:T(8,128)(2,1)S(1)} %get-tuple-element.34), channel_id=1, source_target_pairs={{0,1},{1,0},{2,3},{3,2},{4,5},{5,4},{6,7},{7,6},{8,9},{9,8},{10,11... | collective-permute-start | bytes 368648 | tf_op jit(solution)/shard_map/ppermute | solution.py:420
  16.0 0.7 %join.1 = bf16[24,4,512]{2,1,0:T(4,128)(2,1)} custom-call(f32[96,512]{1,0:T(8,128)S(1)} %get-tuple-element.41.branch, f32[96,512]{1,0:T(8,128)S(1)} %collective-permute-done.6.branch_other, f32[96,512]{1,0:T(8,128)S(1)} %get-tuple-element.43.start, bf16[512]{0:T(512)(128)(2,1)S(1)} %copy-done.8, bf16[1024]{0:T(1024)(128)(2,1)S(1)} %copy-done.3), custom_call_target="tpu_custom_call" | custom-call | tf_op jit(solution)/shard_map/join/pallas_call | solution.py:26
  16.8 5.3 %all-to-all-start = ((bf16[24,4,512]{2,1,0:T(4,128)(2,1)}), bf16[24,4,512]{2,1,0:T(4,128)(2,1)S(1)}, u32[]{:S(2)}, u32[]{:S(2)}) async-start(bf16[24,4,512]{2,1,0:T(4,128)(2,1)} %join.1), calls=%async_computation | async-start | bytes 196608 | tf_op jit(solution)/shard_map/spread/all_to_all | solution.py:429
  22.1 0.2 norm_grad.1
  22.3 1.5 %collective-permute-start.4 = (bf16[72,512]{1,0:T(8,128)(2,1)S(1)}, bf16[72,512]{1,0:T(8,128)(2,1)S(1)}, u32[]{:S(2)}, u32[]{:S(2)}) collective-permute-start(bf16[72,512]{1,0:T(8,128)(2,1)S(1)} %get-tuple-element.39), channel_id=1, source_target_pairs={{0,2},{2,0},{4,6},{6,4},{8,10},{10,8},{12,14},{14,12},{1,3},{3,1},... | collective-permute-start | bytes 221192 | tf_op jit(solution)/shard_map/grad_halo/inner/ppermute | solution.py:330
  23.8 1.9 %collective-permute-start.5 = (bf16[72,512]{1,0:T(8,128)(2,1)S(1)}, bf16[72,512]{1,0:T(8,128)(2,1)S(1)}, u32[]{:S(2)}, u32[]{:S(2)}) collective-permute-start(bf16[72,512]{1,0:T(8,128)(2,1)S(1)} %get-tuple-element.40), channel_id=1, source_target_pairs={{0,0},{2,4},{4,2},{6,8},{8,6},{10,12},{12,10},{14,14},{1,1},{3,5},... | collective-permute-start | bytes 221192 | tf_op jit(solution)/shard_map/grad_halo/outer/ppermute | solution.py:332
  25.8 0.4 %unmix_own.1.part = f32[96,512]{1,0:T(8,128)S(1)} custom-call(f32[96,512]{1,0:T(8,128)S(1)} %get-tuple-element.37.own, f32[8,512]{1,0:T(8,128)S(1)} %get-tuple-element.38.class_rows, f32[56,512]{1,0:T(8,128)S(1)} %get-tuple-element.25.taps), custom_call_target="tpu_custom_call" | custom-call | tf_op jit(solution)/shard_map/unmix_own/pallas_call | solution.py:26
  26.2 0.7 %collective-permute-done.4.inner = bf16[72,512]{1,0:T(8,128)(2,1)S(1)} collective-permute-done((bf16[72,512]{1,0:T(8,128)(2,1)S(1)}, bf16[72,512]{1,0:T(8,128)(2,1)S(1)}, u32[]{:S(2)}, u32[]{:S(2)}) %collective-permute-start.4) | collective-permute-done | bytes 73760 | tf_op jit(solution)/shard_map/grad_halo/inner/ppermute | solution.py:330
  26.9 4.1 %collective-permute-done.5.outer = bf16[72,512]{1,0:T(8,128)(2,1)S(1)} collective-permute-done((bf16[72,512]{1,0:T(8,128)(2,1)S(1)}, bf16[72,512]{1,0:T(8,128)(2,1)S(1)}, u32[]{:S(2)}, u32[]{:S(2)}) %collective-permute-start.5) | collective-permute-done | bytes 73760 | tf_op jit(solution)/shard_map/grad_halo/outer/ppermute | solution.py:332
  31.0 1.1 %unmix_sides.1 = (f32[24,4,512]{2,1,0:T(4,128)}, bf16[3,32,512]{2,1,0:T(8,128)(2,1)}) custom-call(f32[96,512]{1,0:T(8,128)S(1)} %unmix_own.1.part, bf16[72,512]{1,0:T(8,128)(2,1)S(1)} %collective-permute-done.4.inner, bf16[72,512]{1,0:T(8,128)(2,1)S(1)} %collective-permute-done.5.outer, f32[56,512]{1,0:T(8,128)S(1)} %get-tuple-element.25.taps, ...), custom_call_target="tpu_custom_call" | custom-call | tf_op jit(solution)/shard_map/unmix_sides/pallas_call | solution.py:26
  (20 shorter events, 0.0 us)
Async XLA Ops:
  0.6 6.0 %copy-start.1 = (bf16[24,4,512]{2,1,0:T(4,128)(2,1)S(1)}, bf16[24,4,512]{2,1,0:T(4,128)(2,1)}, u32[]{:S(2)}) copy-start(bf16[24,4,512]{2,1,0:T(4,128)(2,1)} %own.1) | copy-start | bytes 294916
  0.6 6.0 %copy-start.6 = (bf16[512]{0:T(512)(128)(2,1)S(1)}, bf16[512]{0:T(512)(128)(2,1)}, u32[]{:S(2)}) copy-start(bf16[512]{0:T(512)(128)(2,1)} %dw_bias.1) | copy-start | bytes 3076
  0.7 6.0 %copy-start.2 = (bf16[7,7,512]{2,1,0:T(8,128)(2,1)S(1)}, bf16[7,7,512]{2,1,0:T(8,128)(2,1)}, u32[]{:S(2)}) copy-start(bf16[7,7,512]{2,1,0:T(8,128)(2,1)} %dw_kernel.1) | copy-start | bytes 150532
  0.7 9.2 %copy-start.5 = (bf16[512]{0:T(512)(128)(2,1)S(1)}, bf16[512]{0:T(512)(128)(2,1)}, u32[]{:S(2)}) copy-start(bf16[512]{0:T(512)(128)(2,1)} %gain.3) | copy-start | bytes 3076
  0.7 9.2 %copy-start.7 = (bf16[512]{0:T(512)(128)(2,1)S(1)}, bf16[512]{0:T(512)(128)(2,1)}, u32[]{:S(2)}) copy-start(bf16[512]{0:T(512)(128)(2,1)} %shift.1) | copy-start | bytes 3076
  0.7 11.2 %copy-start = (bf16[1024,2048]{1,0:T(8,128)(2,1)S(1)}, bf16[1024,2048]{1,0:T(8,128)(2,1)}, u32[]{:S(2)}) copy-start(bf16[1024,2048]{1,0:T(8,128)(2,1)} %up.3) | copy-start | bytes 12582916
  0.7 11.2 %copy-start.4 = (bf16[2048]{0:T(1024)(128)(2,1)S(1)}, bf16[2048]{0:T(1024)(128)(2,1)}, u32[]{:S(2)}) copy-start(bf16[2048]{0:T(1024)(128)(2,1)} %up_bias.1) | copy-start | bytes 12292
  0.7 6.5 %collective-permute-start = (bf16[24,4,512]{2,1,0:T(4,128)(2,1)}, bf16[24,4,512]{2,1,0:T(4,128)(2,1)S(1)}, u32[]{:S(2)}, u32[]{:S(2)}) collective-permute-start(bf16[24,4,512]{2,1,0:T(4,128)(2,1)} %own.1), channel_id=1, source_target_pairs={{0,2},{2,0},{4,6},{6,4},{8,10},{10,8},{12,14},{14,12},{1,3},{3,1},... | collective-permute-start | bytes 294920 | tf_op jit(solution)/shard_map/latent_halo/inner/ppermute | solution.py:330
  2.3 7.6 %collective-permute-start.1 = (bf16[24,4,512]{2,1,0:T(4,128)(2,1)}, bf16[24,4,512]{2,1,0:T(4,128)(2,1)S(1)}, u32[]{:S(2)}, u32[]{:S(2)}) collective-permute-start(bf16[24,4,512]{2,1,0:T(4,128)(2,1)} %own.1), channel_id=1, source_target_pairs={{0,0},{2,4},{4,2},{6,8},{8,6},{10,12},{12,10},{14,14},{1,1},{3,5},... | collective-permute-start | bytes 294920 | tf_op jit(solution)/shard_map/latent_halo/outer/ppermute | solution.py:332
  10.4 1.5 %collective-permute-start.2 = (f32[104,512]{1,0:T(8,128)S(1)}, f32[104,512]{1,0:T(8,128)S(1)}, u32[]{:S(2)}, u32[]{:S(2)}) collective-permute-start(f32[104,512]{1,0:T(8,128)S(1)} %mix_sides.1.own), channel_id=1, source_target_pairs={{0,1},{1,0},{2,3},{3,2},{4,5},{5,4},{6,7},{7,6},{8,9},{9,8},{10,11... | collective-permute-start | bytes 638984 | tf_op jit(solution)/shard_map/ppermute | solution.py:396
  13.8 2.2 %copy-start.3 = (bf16[1024]{0:T(1024)(128)(2,1)S(1)}, bf16[1024]{0:T(1024)(128)(2,1)}, u32[]{:S(2)}) copy-start(bf16[1024]{0:T(1024)(128)(2,1)} %layer_scale.3) | copy-start | bytes 6148
  13.9 2.2 %copy-start.8 = (bf16[512]{0:T(512)(128)(2,1)S(1)}, bf16[512]{0:T(512)(128)(2,1)}, u32[]{:S(2)}) copy-start(bf16[512]{0:T(512)(128)(2,1)} %down_bias.1) | copy-start | bytes 3076
  13.9 2.2 %collective-permute-start.6 = (f32[96,512]{1,0:T(8,128)S(1)}, f32[96,512]{1,0:T(8,128)S(1)}, u32[]{:S(2)}, u32[]{:S(2)}) collective-permute-start(f32[96,512]{1,0:T(8,128)S(1)} %get-tuple-element.42), channel_id=1, source_target_pairs={{0,1},{1,0},{2,3},{3,2},{4,5},{5,4},{6,7},{7,6},{8,9},{9,8},{10,11... | collective-permute-start | bytes 589832 | tf_op jit(solution)/shard_map/ppermute | solution.py:413
  15.7 6.4 %collective-permute-start.3 = (bf16[96,640]{1,0:T(8,128)(2,1)S(1)}, bf16[96,640]{1,0:T(8,128)(2,1)S(1)}, u32[]{:S(2)}, u32[]{:S(2)}) collective-permute-start(bf16[96,640]{1,0:T(8,128)(2,1)S(1)} %get-tuple-element.34), channel_id=1, source_target_pairs={{0,1},{1,0},{2,3},{3,2},{4,5},{5,4},{6,7},{7,6},{8,9},{9,8},{10,11... | collective-permute-start | bytes 368648 | tf_op jit(solution)/shard_map/ppermute | solution.py:420
  16.8 14.2 %all-to-all-start = ((bf16[24,4,512]{2,1,0:T(4,128)(2,1)}), bf16[24,4,512]{2,1,0:T(4,128)(2,1)S(1)}, u32[]{:S(2)}, u32[]{:S(2)}) async-start(bf16[24,4,512]{2,1,0:T(4,128)(2,1)} %join.1), calls=%async_computation | async-start | bytes 196608 | tf_op jit(solution)/shard_map/spread/all_to_all | solution.py:429
  22.3 4.6 %collective-permute-start.4 = (bf16[72,512]{1,0:T(8,128)(2,1)S(1)}, bf16[72,512]{1,0:T(8,128)(2,1)S(1)}, u32[]{:S(2)}, u32[]{:S(2)}) collective-permute-start(bf16[72,512]{1,0:T(8,128)(2,1)S(1)} %get-tuple-element.39), channel_id=1, source_target_pairs={{0,2},{2,0},{4,6},{6,4},{8,10},{10,8},{12,14},{14,12},{1,3},{3,1},... | collective-permute-start | bytes 221192 | tf_op jit(solution)/shard_map/grad_halo/inner/ppermute | solution.py:330
  23.8 7.1 %collective-permute-start.5 = (bf16[72,512]{1,0:T(8,128)(2,1)S(1)}, bf16[72,512]{1,0:T(8,128)(2,1)S(1)}, u32[]{:S(2)}, u32[]{:S(2)}) collective-permute-start(bf16[72,512]{1,0:T(8,128)(2,1)S(1)} %get-tuple-element.40), channel_id=1, source_target_pairs={{0,0},{2,4},{4,2},{6,8},{8,6},{10,12},{12,10},{14,14},{1,1},{3,5},... | collective-permute-start | bytes 221192 | tf_op jit(solution)/shard_map/grad_halo/outer/ppermute | solution.py:332
